TPU v7x, 256 devices: a whole 4x4x8 slice. The times are simulated.
256 devices in a mesh: rep: 32 (over x, z), tp: 8 (over y, core).
Axes of the slice: x: 4, y: 4, z: 8, core: 2. Of those that a mesh axis runs over, the one named last changes fastest.
Arguments:
- hidden_in: bfloat16 [1024, 3584], P('rep'), may hold values from -6 to 6
- k_cache: bfloat16 [1024, 8, 64, 128], P('rep', 'tp'), may hold values from -300 to 300, as said below
- v_cache: bfloat16 [1024, 8, 64, 128], P('rep', 'tp'), may hold values from -6 to 6
- lengths: int32 [1024], replicated, may hold values from 1 to 127, 65536 in all
- routes: int32 [1024, 1], replicated, may hold values from 0 to 31; in each aligned block of 32 rows (0 to 31, 32 to 63, ...) at most 2 rows name the same one
- w_query: bfloat16 [3584, 2048], P(None, 'tp'), may hold values from -0.09375 to 0.09375
- b_query: bfloat16 [2048], P('tp'), may hold values from -3 to 3
- w_key: bfloat16 [3584, 512], P(None, 'tp'), may hold values from -0.09375 to 0.09375
- b_key: bfloat16 [512], P('tp'), may hold values from -3 to 3
- w_value: bfloat16 [3584, 512], P(None, 'tp'), may hold values from -0.09375 to 0.09375
- b_value: bfloat16 [512], P('tp'), may hold values from -3 to 3
- w_out: bfloat16 [2048, 3584], P('tp'), may hold values from -0.125 to 0.125
- gain_in: bfloat16 [3584], replicated, may hold values from 0.25 to 1.75
- gain_out: bfloat16 [3584], replicated, may hold values from 0.25 to 1.75
- w_head: bfloat16 [152064, 3584], P(('rep', 'tp')), may hold values from -0.09375 to 0.09375
Outputs:
- final_norm: float32 [2048], P(('rep', 'tp'))
- top_logit: float32 [2048], P(('rep', 'tp'))
- k_cache_out: bfloat16 [2048, 8, 64, 128], P('rep', 'tp')
- v_cache_out: bfloat16 [2048, 8, 64, 128], P('rep', 'tp')
Inputs may be any that keep to these rules, and one draw needn't show every extreme that they name: `routes`: within the 32 requests of one replica at most 2 name the same replica, and in every draw some replica is named exactly 2 times by some replica's requests. `k_cache`: keys are already rotated to their positions.
All inputs are finite; a program needn't handle non-finite values.
Results may differ from a plain program's by a relative error of at most 0.0022.
Values may be sent and summed in bfloat16 or wider, within the bound.
No kernel may reach another device: no remote copies, remote signals or barrier semaphores. Data moves between devices by JAX's collectives and lax.ppermute only.
A program may use at most 128 MiB of HBM per device.

v0:
```python
import jax
import jax.numpy as jnp
from jax import lax
from jax.sharding import PartitionSpec as P


def swapped(shard, axis, distance):
    return lax.ppermute(shard, axis, [(i, i ^ 1 << distance) for i in range(lax.axis_size(axis))])


def rotate(vals, positions):
    half = vals.shape[-1] // 2
    freq = 1000000.0 ** (-(jnp.arange(half, dtype=jnp.float32) * 2.0 / vals.shape[-1]))
    angle = positions[..., None] * freq
    first = vals[..., :half]
    second = vals[..., half:]
    return jnp.concatenate(
        [
            first * jnp.cos(angle) - second * jnp.sin(angle),
            second * jnp.cos(angle) + first * jnp.sin(angle),
        ],
        axis=-1,
    )


def destinations(routes, n_rep, slots, cap, serve):
    flat = routes[:, 0].reshape(n_rep, slots)
    onehot = (flat[:, :, None] == jnp.arange(n_rep, dtype=jnp.int32)[None, None, :]).astype(
        jnp.int32
    )
    rank = jnp.sum((jnp.cumsum(onehot, axis=1) - onehot) * onehot, axis=2)
    source = jnp.arange(n_rep, dtype=jnp.int32)[:, None]
    return ((flat * serve + source * cap + rank).reshape(-1), flat * cap + rank)


def find_home(dest_flat, targets):
    equal = dest_flat[None, :] == targets[:, None]
    home = jnp.sum(
        jnp.where(equal, jnp.arange(dest_flat.shape[0], dtype=jnp.int32)[None, :], 0), axis=1
    )
    return (home, jnp.any(equal, axis=1))


def fill_buckets(arrays, own_bucket, serve, slots):
    hits = own_bucket[None, :] == jnp.arange(serve, dtype=jnp.int32)[:, None]
    pick = jnp.sum(jnp.where(hits, jnp.arange(slots, dtype=jnp.int32)[None, :], 0), axis=1)
    filled = jnp.any(hits, axis=1)
    return tuple(
        [
            jnp.where(
                filled.reshape((-1,) + (1,) * (item.ndim - 1)),
                item[pick],
                jnp.zeros((), item.dtype),
            )
            for item in arrays
        ]
    )


def write_newest(stored, newest, lens, live_rows, part):
    half_len = stored.shape[1]
    where_pos = part * half_len + jnp.arange(half_len, dtype=jnp.int32)
    written = (where_pos[None, :] == lens[:, None]) & live_rows[:, None]
    return jnp.where(written[:, :, None], newest[:, None, :], stored)


def layer(
    xs,
    keys,
    values,
    lens,
    w_query,
    b_query,
    w_key,
    b_key,
    w_value,
    b_value,
    w_out,
    gain_in,
    gain_out,
    tp_pos,
    n_tp,
):
    eps = 1e-06
    count = xs.shape[0]
    head_size = keys.shape[-1]
    half_len = keys.shape[1]
    part = tp_pos % 2
    even = part == 0
    xf = xs.astype(jnp.float32)
    normed_in = (
        xf * lax.rsqrt(jnp.mean(xf * xf, axis=1, keepdims=True) + eps) * gain_in.astype(jnp.float32)
    ).astype(jnp.bfloat16)
    positions = lens.astype(jnp.float32)[:, None]
    query = (
        jnp.dot(normed_in, w_query, preferred_element_type=jnp.float32)
        + b_query.astype(jnp.float32)
    ).reshape(count, -1, head_size)
    query = rotate(query, positions).astype(jnp.bfloat16)
    key_part = (
        jnp.dot(normed_in, w_key, preferred_element_type=jnp.float32) + b_key.astype(jnp.float32)
    ).astype(jnp.bfloat16)
    value_part = (
        jnp.dot(normed_in, w_value, preferred_element_type=jnp.float32)
        + b_value.astype(jnp.float32)
    ).astype(jnp.bfloat16)
    other_query, other_key, other_value = swapped((query, key_part, value_part), "tp", 0)
    queries = jnp.where(
        even,
        jnp.concatenate([query, other_query], axis=1),
        jnp.concatenate([other_query, query], axis=1),
    )
    key_raw = jnp.where(
        even,
        jnp.concatenate([key_part, other_key], axis=1),
        jnp.concatenate([other_key, key_part], axis=1),
    )
    value_new = jnp.where(
        even,
        jnp.concatenate([value_part, other_value], axis=1),
        jnp.concatenate([other_value, value_part], axis=1),
    )
    key_new = rotate(key_raw.astype(jnp.float32)[:, None, :], positions)[:, 0].astype(jnp.bfloat16)
    scale = 1.0 / head_size**0.5
    scores = jnp.einsum("sgd,spd->sgp", queries, keys, preferred_element_type=jnp.float32) * scale
    place = part * half_len + jnp.arange(half_len, dtype=jnp.int32)
    live = (place[None, :] < lens[:, None])[:, None, :]
    scores = jnp.where(live, scores, -1e30)
    own_score = (
        jnp.einsum("sgd,sd->sg", queries, key_new, preferred_element_type=jnp.float32) * scale
    )
    own_score = jnp.where(even, own_score, -1e30)
    peak = jnp.maximum(jnp.max(scores, axis=2), own_score)
    weights = jnp.where(live, jnp.exp(scores - peak[..., None]), 0.0)
    own_weight = jnp.where(even, jnp.exp(own_score - peak), 0.0)
    total = jnp.sum(weights, axis=2) + own_weight
    mixed = jnp.einsum(
        "sgp,spd->sgd", weights, values.astype(jnp.float32), precision=lax.Precision.HIGHEST
    )
    mixed = mixed + own_weight[..., None] * value_new.astype(jnp.float32)[:, None, :]
    mixed_keep = jnp.where(even, mixed[:, :2], mixed[:, 2:])
    mixed_give = jnp.where(even, mixed[:, 2:], mixed[:, :2])
    peak_keep = jnp.where(even, peak[:, :2], peak[:, 2:])
    peak_give = jnp.where(even, peak[:, 2:], peak[:, :2])
    total_keep = jnp.where(even, total[:, :2], total[:, 2:])
    total_give = jnp.where(even, total[:, 2:], total[:, :2])
    got_mixed, got_peak, got_total = swapped((mixed_give, peak_give, total_give), "tp", 0)
    upper = jnp.maximum(peak_keep, got_peak)
    mine = jnp.exp(peak_keep - upper)
    theirs = jnp.exp(got_peak - upper)
    merged = (mixed_keep * mine[..., None] + got_mixed * theirs[..., None]) / (
        total_keep * mine + got_total * theirs
    )[..., None]
    attn = merged.reshape(count, -1).astype(jnp.bfloat16)
    rows = count // n_tp
    projected = lax.psum_scatter(
        jnp.dot(attn, w_out, preferred_element_type=jnp.float32),
        "tp",
        scatter_dimension=0,
        tiled=True,
    )
    own_x = lax.dynamic_slice_in_dim(xf, tp_pos * rows, rows, 0)
    state = (own_x + projected).astype(jnp.bfloat16)
    sf = state.astype(jnp.float32)
    ms = jnp.mean(sf * sf, axis=1)
    normed = (sf * lax.rsqrt(ms + eps)[:, None] * gain_out.astype(jnp.float32)).astype(jnp.bfloat16)
    return (normed, jnp.sqrt(ms), rows, key_new, value_new)


def per_device(
    hidden_in,
    k_cache,
    v_cache,
    lengths,
    routes,
    w_query,
    b_query,
    w_key,
    b_key,
    w_value,
    b_value,
    w_out,
    gain_in,
    gain_out,
    w_head,
):
    n_rep = lax.axis_size("rep")
    n_tp = lax.axis_size("tp")
    rep_pos = lax.axis_index("rep")
    tp_pos = lax.axis_index("tp")
    part = tp_pos % 2
    slots = hidden_in.shape[0]
    cap = max(2, 2 * slots // n_rep)
    serve = n_rep * cap
    dest_flat, bucket_grid = destinations(routes, n_rep, slots, cap, serve)
    own_bucket = lax.dynamic_slice_in_dim(bucket_grid, rep_pos, 1, 0)[0]
    keys_home = k_cache[:, 0]
    values_home = v_cache[:, 0]
    weights_all = (w_query, b_query, w_key, b_key, w_value, b_value, w_out, gain_in, gain_out)
    send_x, send_k, send_v = fill_buckets(
        (hidden_in, keys_home, values_home), own_bucket, serve, slots
    )
    got_x, got_k, got_v = (
        lax.all_to_all(send_x, "rep", split_axis=0, concat_axis=0, tiled=True),
        lax.all_to_all(send_k, "rep", split_axis=0, concat_axis=0, tiled=True),
        lax.all_to_all(send_v, "rep", split_axis=0, concat_axis=0, tiled=True),
    )
    targets = rep_pos * serve + jnp.arange(serve, dtype=jnp.int32)
    home, valid = find_home(dest_flat, targets)
    lens = jnp.where(valid, lengths[home], 0)
    normed, norm_own, rows, key_new, value_new = layer(
        got_x, got_k, got_v, lens, *weights_all, tp_pos, n_tp
    )
    keys_served = write_newest(got_k, key_new, lens, valid, part)
    values_served = write_newest(got_v, value_new, lens, valid, part)
    logits = lax.dot_general(
        lax.all_gather(normed, ("rep", "tp"), axis=0, tiled=True),
        w_head,
        (((1,), (1,)), ((), ())),
        preferred_element_type=jnp.float32,
    )
    partial_value = jnp.max(logits, axis=1)
    top_all = lax.pmax(partial_value, ("rep", "tp"))
    own_valid = lax.dynamic_slice_in_dim(valid, tp_pos * rows, rows, 0)
    top_own = lax.dynamic_slice_in_dim(top_all, (rep_pos * n_tp + tp_pos) * rows, rows, 0)
    final_norm = jnp.where(own_valid, norm_own, 0.0)
    top_logit = jnp.where(own_valid, top_own, 0.0)
    return (final_norm, top_logit, keys_served[:, None], values_served[:, None])


def solution(mesh):
    in_specs = (
        P("rep", None),
        P("rep", "tp", None, None),
        P("rep", "tp", None, None),
        P(),
        P(),
        P(None, "tp"),
        P("tp"),
        P(None, "tp"),
        P("tp"),
        P(None, "tp"),
        P("tp"),
        P("tp", None),
        P(),
        P(),
        P(("rep", "tp"), None),
    )
    out_specs = (
        P(("rep", "tp")),
        P(("rep", "tp")),
        P("rep", "tp", None, None),
        P("rep", "tp", None, None),
    )
    return jax.shard_map(
        per_device, mesh=mesh, in_specs=in_specs, out_specs=out_specs, check_vma=False
    )
```

profile of v0, /device:TPU:1, one launch (start us, length us, event | category | flops | bytes accessed | tf_op | source)
XLA Modules:
  0.0 368.8 jit_solution(1046616526349148043)
XLA Ops:
  7.8 1.3 broadcast_multiply_fusion
  9.3 1.0 fusion.42
  11.3 2.3 gather_fusion
  13.8 1.3 broadcast_select_fusion.2
  15.0 12.0 %all-to-all-start = ((bf16[32,2,3584]{2,1,0:T(2,128)(2,1)}), bf16[32,2,3584]{2,1,0:T(2,128)(2,1)}, u32[]{:S(2)}, u32[]{:S(2)}) async-start(bf16[32,2,3584]{2,1,0:T(2,128)(2,1)} %broadcast_select_fusion.2), calls=%async_computation | async-start | bytes 917504 | tf_op jit(solution)/shard_map/all_to_all | solution.py:204
  29.7 2.7 gather_fusion.2
  33.4 2.8 broadcast_select_fusion.1
  36.3 3.7 all-to-all-done
  39.9 7.8 %all-to-all-start.1 = ((bf16[64,64,128]{2,1,0:T(8,128)(2,1)}), bf16[64,64,128]{2,1,0:T(8,128)(2,1)S(1)}, u32[]{:S(2)}, u32[]{:S(2)}) async-start(bf16[64,64,128]{2,1,0:T(8,128)(2,1)} %get-tuple-element.49), calls=%async_computation.1 | async-start | bytes 2097152 | tf_op jit(solution)/shard_map/all_to_all | solution.py:205
  47.7 1.6 multiply_reduce_fusion
  49.4 2.1 reshape.425
  51.5 1.3 multiply_convert_fusion
  52.8 1.9 convolution_add_fusion.1
  54.8 1.3 fusion.1
  56.1 1.4 collective-permute-start.1
  57.5 1.3 fusion.2
  59.8 12.7 %all-to-all-done.1 = bf16[64,64,128]{2,1,0:T(8,128)(2,1)S(1)} async-done(((bf16[64,64,128]{2,1,0:T(8,128)(2,1)}), bf16[64,64,128]{2,1,0:T(8,128)(2,1)S(1)}, u32[]{:S(2)}, u32[]{:S(2)}) %all-to-all-start.1) | async-done | bytes 1048608 | tf_op jit(solution)/shard_map/all_to_all | solution.py:205
  72.5 8.5 %all-to-all-start.2 = ((bf16[64,64,128]{2,1,0:T(8,128)(2,1)}), bf16[64,64,128]{2,1,0:T(8,128)(2,1)}, u32[]{:S(2)}, u32[]{:S(2)}) async-start(bf16[64,64,128]{2,1,0:T(8,128)(2,1)} %get-tuple-element.50), calls=%async_computation.2 | async-start | bytes 2097152 | tf_op jit(solution)/shard_map/all_to_all | solution.py:206
  81.3 0.8 fusion.20
  82.6 0.8 fusion.43
  83.5 1.5 collective-permute-start.3
  85.5 20.3 %all-to-all-done.2 = bf16[64,64,128]{2,1,0:T(8,128)(2,1)} async-done(((bf16[64,64,128]{2,1,0:T(8,128)(2,1)}), bf16[64,64,128]{2,1,0:T(8,128)(2,1)}, u32[]{:S(2)}, u32[]{:S(2)}) %all-to-all-start.2) | async-done | bytes 1048608 | tf_op jit(solution)/shard_map/all_to_all | solution.py:206
  105.8 2.2 convolution_add_fusion
  108.1 5.1 %collective-permute-start.4 = (f32[64,2,128]{2,1,0:T(2,128)S(1)}, f32[64,2,128]{2,1,0:T(2,128)S(1)}, u32[]{:S(2)}, u32[]{:S(2)}) collective-permute-start(f32[64,2,128]{2,1,0:T(2,128)S(1)} %broadcast_select_fusion.3), channel_id=1, source_target_pairs={{0,1},{1,0},{2,3},{3,2},{4,5},{5,4},{6,7},{7,6},{8,9},{9,8},{10,11... | collective-permute-start | bytes 196616 | tf_op jit(solution)/shard_map/ppermute | solution.py:8
  113.3 0.8 collective-permute-done.4
  114.3 1.4 fusion.25
  115.8 28.0 %reduce-scatter.2.cloned.1.call-done = f32[8,3584]{1,0:T(8,128)} async-done(((f32[64,3584]{1,0:T(8,128)}), f32[8,3584]{1,0:T(8,128)}) %reduce-scatter.2.cloned.1.call-update) | async-done | bytes 114704 | tf_op jit(solution)/shard_map/reduce_scatter | solution.py:156
  143.8 1.1 fusion.7
  145.8 3.6 select_bitcast_fusion
  149.4 123.5 %all-gather.2.cloned.1.call-done = bf16[2048,3584]{1,0:T(8,128)(2,1)} async-done(((bf16[8,3584]{1,0:T(8,128)(2,1)}), bf16[2048,3584]{1,0:T(8,128)(2,1)}) %all-gather.2.cloned.1.call-update) | async-done | bytes 14680080 | tf_op jit(solution)/shard_map/all_gather | solution.py:217
  272.9 13.6 %convolution_reduce_fusion = f32[2048]{0:T(1024)S(1)} fusion(bf16[2048,3584]{1,0:T(8,128)(2,1)} %all-gather.2.cloned.1.call-done, bf16[594,3584]{1,0:T(8,128)(2,1)} %param.29), kind=kOutput, calls=%fused_computation.4 | convolution fusion | flops 8721172480 | bytes 18946048 | tf_op jit(solution)/shard_map/dot_general | solution.py:216
  286.5 74.8 %pmax.7 = f32[2048]{0:T(1024)S(1)} all-reduce(f32[2048]{0:T(1024)S(1)} %convolution_reduce_fusion), channel_id=1, replica_groups=mesh['rep'=32,'tp'=8] {'rep','tp'}, use_global_device_ids=true, to_apply=%region_12.13 | all-reduce | flops 2048 | bytes 16384 | tf_op jit(solution)/shard_map/pmax | solution.py:223
  (91 shorter events, 9.8 us)
Async XLA Ops:
  7.2 107.2 %copy-start = (bf16[256,3584]{1,0:T(8,128)(2,1)S(1)}, bf16[256,3584]{1,0:T(8,128)(2,1)}, u32[]{:S(2)}) copy-start(bf16[256,3584]{1,0:T(8,128)(2,1)} %param.26) | copy-start | bytes 5505028
  7.2 20.1 %copy-start.10 = (bf16[64]{0:T(256)(128)(2,1)S(1)}, bf16[64]{0:T(256)(128)(2,1)}, u32[]{:S(2)}) copy-start(bf16[64]{0:T(256)(128)(2,1)} %param.23) | copy-start | bytes 388
  7.2 20.6 %copy-start.11 = (bf16[64]{0:T(256)(128)(2,1)S(1)}, bf16[64]{0:T(256)(128)(2,1)}, u32[]{:S(2)}) copy-start(bf16[64]{0:T(256)(128)(2,1)} %param.25) | copy-start | bytes 388
  7.2 21.1 %copy-start.12 = (bf16[256]{0:T(256)(128)(2,1)S(1)}, bf16[256]{0:T(256)(128)(2,1)}, u32[]{:S(2)}) copy-start(bf16[256]{0:T(256)(128)(2,1)} %param.21) | copy-start | bytes 1540
  7.2 21.7 %copy-start.3 = (bf16[3584]{0:T(1024)(128)(2,1)S(1)}, bf16[3584]{0:T(1024)(128)(2,1)}, u32[]{:S(2)}) copy-start(bf16[3584]{0:T(1024)(128)(2,1)} %param.27) | copy-start | bytes 21508
  7.2 21.7 %copy-start.2 = (bf16[32,1,64,128]{3,2,1,0:T(8,128)(2,1)S(1)}, bf16[32,1,64,128]{3,2,1,0:T(8,128)(2,1)}, u32[]{:S(2)}) copy-start(bf16[32,1,64,128]{3,2,1,0:T(8,128)(2,1)} %param.17) | copy-start | bytes 1572868
  13.6 18.8 %copy-start.1 = (s32[1024]{0:T(1024)S(1)}, s32[1024]{0:T(1024)}, u32[]{:S(2)}) copy-start(s32[1024]{0:T(1024)} %param.18) | copy-start | bytes 12292
  15.0 24.9 %all-to-all-start = ((bf16[32,2,3584]{2,1,0:T(2,128)(2,1)}), bf16[32,2,3584]{2,1,0:T(2,128)(2,1)}, u32[]{:S(2)}, u32[]{:S(2)}) async-start(bf16[32,2,3584]{2,1,0:T(2,128)(2,1)} %broadcast_select_fusion.2), calls=%async_computation | async-start | bytes 917504 | tf_op jit(solution)/shard_map/all_to_all | solution.py:204
  27.1 9.2 %copy-start.8 = (f32[64]{0:T(128)}, f32[64]{0:T(128)S(1)}, u32[]{:S(2)}) copy-start(f32[64]{0:T(128)S(1)} %negate_power_fusion) | copy-start | bytes 772
  27.3 9.0 %copy-start.5 = (pred[64]{0:T(512)(128)(4,1)}, pred[64]{0:T(512)(128)(4,1)S(1)}, u32[]{:S(2)}) copy-start(pred[64]{0:T(512)(128)(4,1)S(1)} %compare_reduce_fusion) | copy-start | bytes 196
  33.1 14.6 %copy-start.7 = (f32[64]{0:T(128)}, f32[64]{0:T(128)S(1)}, u32[]{:S(2)}) copy-start(f32[64]{0:T(128)S(1)} %get-tuple-element.33) | copy-start | bytes 772
  33.4 19.4 %copy-start.9 = (f32[256]{0:T(256)S(1)}, f32[256]{0:T(256)}, u32[]{:S(2)}) copy-start(f32[256]{0:T(256)} %convert_element_type.91) | copy-start | bytes 3076
  39.9 32.6 %all-to-all-start.1 = ((bf16[64,64,128]{2,1,0:T(8,128)(2,1)}), bf16[64,64,128]{2,1,0:T(8,128)(2,1)S(1)}, u32[]{:S(2)}, u32[]{:S(2)}) async-start(bf16[64,64,128]{2,1,0:T(8,128)(2,1)} %get-tuple-element.49), calls=%async_computation.1 | async-start | bytes 2097152 | tf_op jit(solution)/shard_map/all_to_all | solution.py:205
  56.1 25.0 %collective-permute-start.1 = (bf16[64,64]{1,0:T(8,128)(2,1)S(1)}, bf16[64,64]{1,0:T(8,128)(2,1)S(1)}, u32[]{:S(2)}, u32[]{:S(2)}) collective-permute-start(bf16[64,64]{1,0:T(8,128)(2,1)S(1)} %fusion.1), channel_id=1, source_target_pairs={{0,1},{1,0},{2,3},{3,2},{4,5},{5,4},{6,7},{7,6},{8,9},{9,8},{10,11... | collective-permute-start | bytes 24584 | tf_op jit(solution)/shard_map/ppermute | solution.py:8
  58.8 22.4 %collective-permute-start.2 = (bf16[64,64]{1,0:T(8,128)(2,1)S(1)}, bf16[64,64]{1,0:T(8,128)(2,1)S(1)}, u32[]{:S(2)}, u32[]{:S(2)}) collective-permute-start(bf16[64,64]{1,0:T(8,128)(2,1)S(1)} %fusion.2), channel_id=1, source_target_pairs={{0,1},{1,0},{2,3},{3,2},{4,5},{5,4},{6,7},{7,6},{8,9},{9,8},{10,11... | collective-permute-start | bytes 24584 | tf_op jit(solution)/shard_map/ppermute | solution.py:8
  59.2 23.0 %collective-permute-start = (bf16[64,2,128]{2,1,0:T(2,128)(2,1)S(1)}, bf16[64,2,128]{2,1,0:T(2,128)(2,1)S(1)}, u32[]{:S(2)}, u32[]{:S(2)}) collective-permute-start(bf16[64,2,128]{2,1,0:T(2,128)(2,1)S(1)} %pad_maximum_fusion), channel_id=1, source_target_pairs={{0,1},{1,0},{2,3},{3,2},{4,5},{5,4},{6,7},{7,6},{8,9},{9,8},{10,11... | collective-permute-start | bytes 98312 | tf_op jit(solution)/shard_map/ppermute | solution.py:8
  72.5 33.3 %all-to-all-start.2 = ((bf16[64,64,128]{2,1,0:T(8,128)(2,1)}), bf16[64,64,128]{2,1,0:T(8,128)(2,1)}, u32[]{:S(2)}, u32[]{:S(2)}) async-start(bf16[64,64,128]{2,1,0:T(8,128)(2,1)} %get-tuple-element.50), calls=%async_computation.2 | async-start | bytes 2097152 | tf_op jit(solution)/shard_map/all_to_all | solution.py:206
  81.1 62.8 %reduce-scatter.2.cloned.1.call-start = ((), (), s32[]{:S(2)}) async-start(), calls=%async_computation.4 | async-start | bytes 1032192 | tf_op jit(solution)/shard_map/reduce_scatter | solution.py:156
  82.6 33.2 %copy-start.4 = (bf16[3584]{0:T(1024)(128)(2,1)S(1)}, bf16[3584]{0:T(1024)(128)(2,1)}, u32[]{:S(2)}) copy-start(bf16[3584]{0:T(1024)(128)(2,1)} %param.28) | copy-start | bytes 21508
  83.5 29.7 %collective-permute-start.3 = (f32[64,2]{1,0:T(8,128)S(1)}, f32[64,2]{1,0:T(8,128)S(1)}, u32[]{:S(2)}, u32[]{:S(2)}) collective-permute-start(f32[64,2]{1,0:T(8,128)S(1)} %slice_select_fusion.1), channel_id=1, source_target_pairs={{0,1},{1,0},{2,3},{3,2},{4,5},{5,4},{6,7},{7,6},{8,9},{9,8},{10,11... | collective-permute-start | bytes 1544 | tf_op jit(solution)/shard_map/ppermute | solution.py:8
  85.3 27.9 %collective-permute-start.5 = (f32[64,2]{1,0:T(8,128)S(1)}, f32[64,2]{1,0:T(8,128)S(1)}, u32[]{:S(2)}, u32[]{:S(2)}) collective-permute-start(f32[64,2]{1,0:T(8,128)S(1)} %slice_select_fusion), channel_id=1, source_target_pairs={{0,1},{1,0},{2,3},{3,2},{4,5},{5,4},{6,7},{7,6},{8,9},{9,8},{10,11... | collective-permute-start | bytes 1544 | tf_op jit(solution)/shard_map/ppermute | solution.py:8
  108.1 6.0 %collective-permute-start.4 = (f32[64,2,128]{2,1,0:T(2,128)S(1)}, f32[64,2,128]{2,1,0:T(2,128)S(1)}, u32[]{:S(2)}, u32[]{:S(2)}) collective-permute-start(f32[64,2,128]{2,1,0:T(2,128)S(1)} %broadcast_select_fusion.3), channel_id=1, source_target_pairs={{0,1},{1,0},{2,3},{3,2},{4,5},{5,4},{6,7},{7,6},{8,9},{9,8},{10,11... | collective-permute-start | bytes 196616 | tf_op jit(solution)/shard_map/ppermute | solution.py:8
  115.7 157.1 %all-gather.2.cloned.1.call-start = ((), (), s32[]{:S(2)}) async-start(), calls=%async_computation.5 | async-start | bytes 14737408 | tf_op jit(solution)/shard_map/all_gather | solution.py:217
  149.4 212.0 %copy-start.6 = (pred[64]{0:T(512)(128)(4,1)S(1)}, pred[64]{0:T(512)(128)(4,1)}, u32[]{:S(2)}) copy-start(pred[64]{0:T(512)(128)(4,1)} %copy-done.5) | copy-start | bytes 196
Sparse Core Ops, SparseCore 0:
  115.9 27.9 reduce-scatter.1
  148.0 124.8 all-gather.1
where the time goes:
time: 370 us; the launch traced here: 369 us
  waiting for transfers between devices  189 us (51%)
  blocking collectives  74.8 us (20%)
  starting transfers between devices  37.3 us (10%)
  matrix products  22.9 us (6%)
  other arithmetic  20.3 us (5%)
  between operations  14.5 us (4%)
  local copies, waits for them, and re-layouts  9.94 us (3%)
    all_gather x1, waiting for transfers between devices, per_device(): lax.all_gather(normed, ('rep', 'tp'), axis=0, tiled=True)  123 us
    pmax x1, blocking collectives, per_device(): top_all = lax.pmax(partial_value, ('rep', 'tp'))  74.8 us
    reduce_scatter x1, waiting for transfers between devices, layer(): lax.psum_scatter(jnp.dot(attn, w_out, preferred_element_type=jnp.float32)...  28 us
    all_to_all x1, waiting for transfers between devices, per_device(): lax.all_to_all(send_v, 'rep', split_axis=0, concat_axis=0, tiled=True)  20.3 us
    dot_general x1, matrix products, per_device(): lax.dot_general(lax.all_gather(normed, ('rep', 'tp'), axis=0, tiled=True)...  13.6 us
    all_to_all x1, waiting for transfers between devices, per_device(): lax.all_to_all(send_k, 'rep', split_axis=0, concat_axis=0, tiled=True)  12.7 us
    all_to_all x1, starting transfers between devices, per_device(): lax.all_to_all(send_x, 'rep', split_axis=0, concat_axis=0, tiled=True)  12 us
    ppermute x6, starting transfers between devices, swapped(): lax.ppermute(shard, axis, [(i, i ^ 1 << distance) for i in range(lax.axis...  8.9 us
  transfers between devices with their start and end apart: 11, of which 6 were waited for; matrix products, arithmetic and copies ran while one was open for 8% of the time, Pallas kernels for 0%

commit v1 on v0

v1 whole, which is shorter than its diff:
```python
import jax
import jax.numpy as jnp
from jax import lax
from jax.sharding import Mesh, PartitionSpec as P

REP = ("x", "z")
TP = ("y", "c")
ALL = ("x", "z", "y", "c")


def shifted(value, axis, distance):
    size = lax.axis_size(axis)
    return lax.ppermute(value, axis, [((i + distance) % size, i) for i in range(size)])


def spread(value, axis):
    size = lax.axis_size(axis)
    copies = jnp.broadcast_to(value[None], (size,) + value.shape)
    return lax.all_to_all(copies, axis, split_axis=0, concat_axis=0, tiled=True)


def rotate(vals, cos, sin):
    half = vals.shape[-1] // 2
    first = vals[..., :half]
    second = vals[..., half:]
    return jnp.concatenate([first * cos - second * sin, second * cos + first * sin], axis=-1)


def per_device(
    hidden_in,
    k_cache,
    v_cache,
    lengths,
    routes,
    w_query,
    b_query,
    w_key,
    b_key,
    w_value,
    b_value,
    w_out,
    gain_in,
    gain_out,
    w_head,
):
    f32 = jnp.float32
    bf16 = jnp.bfloat16
    eps = 1e-06
    n_z = lax.axis_size("z")
    n_y = lax.axis_size("y")
    n_rep = lax.axis_size("x") * n_z
    n_tp = n_y * 2
    y_pos = lax.axis_index("y")
    c_pos = lax.axis_index("c")
    rep_pos = lax.axis_index("x") * n_z + lax.axis_index("z")
    even = c_pos == 0
    slots, width = hidden_in.shape
    half_len, head_size = k_cache.shape[2:]
    cap = 2
    serve = n_rep * cap
    cols = width // n_y
    rows = slots // 2

    scaled = (w_head.astype(f32) * gain_out.astype(f32)[None, :]).astype(bf16)
    head = jnp.concatenate([scaled, shifted(scaled, "c", 1)], axis=0)
    head_parts = [
        lax.dynamic_slice_in_dim(head, ((y_pos + d) % n_y) * cols, cols, 1) for d in range(n_y)
    ]

    flat = routes[:, 0].reshape(n_rep, slots)
    earlier = (flat[:, None, :] == flat[:, :, None]) & (
        jnp.arange(slots)[None, None, :] < jnp.arange(slots)[None, :, None]
    )
    rank = jnp.sum(earlier.astype(jnp.int32), axis=2)
    bucket = flat * cap + rank
    own_bucket = lax.dynamic_slice_in_dim(bucket, rep_pos, 1, 0)[0]
    lens = lax.dynamic_slice_in_dim(lengths, rep_pos * slots, slots, 0)

    xf = hidden_in.astype(f32)
    normed_in = (
        xf * lax.rsqrt(jnp.mean(xf * xf, axis=1, keepdims=True) + eps) * gain_in.astype(f32)
    ).astype(bf16)
    half = head_size // 2
    freq = 1000000.0 ** (-(jnp.arange(half, dtype=f32) * 2.0 / head_size))
    angle = lens.astype(f32)[:, None] * freq
    cos, sin = jnp.cos(angle), jnp.sin(angle)
    query = (
        jnp.dot(normed_in, w_query, preferred_element_type=f32) + b_query.astype(f32)
    ).reshape(slots, -1, head_size)
    query = rotate(query, cos[:, None], sin[:, None]).astype(bf16)
    key_part = (jnp.dot(normed_in, w_key, preferred_element_type=f32) + b_key.astype(f32)).astype(
        bf16
    )
    value_part = (
        jnp.dot(normed_in, w_value, preferred_element_type=f32) + b_value.astype(f32)
    ).astype(bf16)
    packed = jnp.concatenate([query.reshape(slots, -1), key_part, value_part], axis=1)
    other = shifted(packed, "c", 1)
    first = jnp.where(even, packed, other)
    second = jnp.where(even, other, packed)
    q_width = query.shape[1] * head_size
    k_width = key_part.shape[1]
    queries = jnp.concatenate([first[:, :q_width], second[:, :q_width]], axis=1).reshape(
        slots, -1, head_size
    )
    key_raw = jnp.concatenate(
        [first[:, q_width : q_width + k_width], second[:, q_width : q_width + k_width]], axis=1
    )
    value_new = jnp.concatenate(
        [first[:, q_width + k_width :], second[:, q_width + k_width :]], axis=1
    )
    key_new = rotate(key_raw.astype(f32), cos, sin).astype(bf16)

    keys = k_cache[:, 0]
    values = v_cache[:, 0]
    scale = 1.0 / head_size**0.5
    scores = jnp.einsum("sgd,spd->sgp", queries, keys, preferred_element_type=f32) * scale
    place = c_pos * half_len + jnp.arange(half_len, dtype=jnp.int32)
    live = (place[None, :] < lens[:, None])[:, None, :]
    scores = jnp.where(live, scores, -1e30)
    own_score = (
        jnp.sum(queries.astype(f32) * key_new.astype(f32)[:, None, :], axis=2) * scale
    )
    own_score = jnp.where(even, own_score, -1e30)
    peak = jnp.maximum(jnp.max(scores, axis=2), own_score)
    weights = jnp.where(live, jnp.exp(scores - peak[..., None]), 0.0)
    own_weight = jnp.where(even, jnp.exp(own_score - peak), 0.0)
    total = jnp.sum(weights, axis=2) + own_weight
    mixed = jnp.einsum("sgp,spd->sgd", weights.astype(bf16), values, preferred_element_type=f32)
    mixed = mixed + own_weight[..., None] * value_new.astype(f32)[:, None, :]
    state_all = jnp.concatenate(
        [
            mixed,
            jnp.broadcast_to(peak[..., None], peak.shape + (head_size,)),
            jnp.broadcast_to(total[..., None], total.shape + (head_size,)),
        ],
        axis=2,
    )
    keep = jnp.where(even, state_all[:, :2], state_all[:, 2:])
    give = jnp.where(even, state_all[:, 2:], state_all[:, :2])
    got = shifted(give, "c", 1)
    peak_keep = keep[..., head_size : head_size + 1]
    peak_got = got[..., head_size : head_size + 1]
    upper = jnp.maximum(peak_keep, peak_got)
    mine = jnp.exp(peak_keep - upper)
    theirs = jnp.exp(peak_got - upper)
    merged = (keep[..., :head_size] * mine + got[..., :head_size] * theirs) / (
        keep[..., 2 * head_size : 2 * head_size + 1] * mine
        + got[..., 2 * head_size : 2 * head_size + 1] * theirs
    )
    attn = merged.reshape(slots, -1).astype(bf16)

    partial = jnp.dot(attn, w_out, preferred_element_type=f32).astype(bf16)
    partial = partial.reshape(2, rows, n_y, cols).transpose(2, 0, 1, 3).reshape(n_tp, rows, cols)
    shares = lax.all_to_all(partial, TP, split_axis=0, concat_axis=0, tiled=True)
    own_x = lax.dynamic_slice(hidden_in, (c_pos * rows, y_pos * cols), (rows, cols))
    state = (own_x.astype(f32) + jnp.sum(shares.astype(f32), axis=0)).astype(bf16)

    gathered = spread(state, "z").reshape(n_z * rows, cols)
    gathered = spread(gathered, "x").reshape(n_rep * rows, cols)
    chunks = [gathered] + [shifted(gathered, "y", d) for d in range(1, n_y)]
    logits = 0.0
    squares = 0.0
    for chunk, weight in zip(chunks, head_parts):
        logits = logits + lax.dot_general(
            chunk, weight, (((1,), (1,)), ((), ())), preferred_element_type=f32
        )
        wide = chunk.astype(f32)
        squares = squares + jnp.sum(wide * wide, axis=1)
    ms = squares / width
    best = (jnp.max(logits, axis=1) * lax.rsqrt(ms + eps)).reshape(n_rep, 1, rows)
    rms = jnp.sqrt(ms).reshape(n_rep, 1, rows)

    own_rows = lax.dynamic_slice(bucket, (0, c_pos * rows), (n_rep, rows))
    hit = own_rows[:, None, :] == jnp.arange(serve, dtype=jnp.int32)[None, :, None]
    send_best = jnp.max(jnp.where(hit, best, -jnp.inf), axis=2)
    send_rms = jnp.max(jnp.where(hit, rms, -1.0), axis=2)
    send = jnp.stack([send_best, send_rms], axis=0).reshape(2, n_rep, n_rep, cap)
    send = send.transpose(2, 1, 0, 3).reshape(n_rep, n_tp, n_rep // n_tp, 2, cap)
    send = send.reshape(n_rep * n_tp, -1)
    arrived = jnp.max(lax.all_to_all(send, ALL, split_axis=0, concat_axis=0, tiled=True), axis=0)
    arrived = arrived.reshape(n_rep // n_tp, 2, cap)
    arrived_best = arrived[:, 0].reshape(-1)
    arrived_rms = arrived[:, 1].reshape(-1)
    taken = arrived_rms >= 0.0
    final_norm = jnp.where(taken, arrived_rms, 0.0)
    top_logit = jnp.where(taken, arrived_best, 0.0)

    written = (place[None, :] == lens[:, None])[:, :, None]
    keys_full = jnp.where(written, key_new[:, None, :], keys)
    values_full = jnp.where(written, value_new[:, None, :], values)
    hits = own_bucket[None, :] == jnp.arange(serve, dtype=jnp.int32)[:, None]
    pick = jnp.sum(jnp.where(hits, jnp.arange(slots, dtype=jnp.int32)[None, :], 0), axis=1)
    filled = jnp.any(hits, axis=1)[:, None, None]
    send_k = jnp.where(filled, keys_full[pick], jnp.zeros((), bf16))
    send_v = jnp.where(filled, values_full[pick], jnp.zeros((), bf16))
    got_k = lax.all_to_all(send_k, REP, split_axis=0, concat_axis=0, tiled=True)
    got_v = lax.all_to_all(send_v, REP, split_axis=0, concat_axis=0, tiled=True)
    return (final_norm, top_logit, got_k[:, None], got_v[:, None])


def solution(mesh):
    n_rep, n_tp = mesh.devices.shape
    fine = Mesh(mesh.devices.reshape(4, n_rep // 4, n_tp // 2, 2), ("x", "z", "y", "c"))
    in_specs = (
        P(REP, None),
        P(REP, TP, None, None),
        P(REP, TP, None, None),
        P(),
        P(),
        P(None, TP),
        P(TP),
        P(None, TP),
        P(TP),
        P(None, TP),
        P(TP),
        P(TP, None),
        P(),
        P(),
        P(ALL, None),
    )
    out_specs = (P(ALL), P(ALL), P(REP, TP, None, None), P(REP, TP, None, None))
    return jax.shard_map(
        per_device, mesh=fine, in_specs=in_specs, out_specs=out_specs, check_vma=False
    )
```

time: 370 us -> 184 us (0.50)
  waiting for transfers between devices: 189 us -> 79 us
  blocking collectives: 74.8 us -> 0 us
  between operations: 14.5 us -> 1.14 us
  starting transfers between devices: 37.3 us -> 46.7 us
  local copies, waits for them, and re-layouts: 9.94 us -> 16.5 us
  matrix products: 22.9 us -> 17 us
    all_gather x1 -> x0, waiting for transfers between devices: 123 us -> none  [per_device(): lax.all_gather(normed, ('rep', 'tp'), axis=0, tiled=True)]
    pmax x1 -> x0, blocking collectives: 74.8 us -> none  [per_device(): top_all = lax.pmax(partial_value, ('rep', 'tp'))]
    ppermute x6, waiting for transfers between devices: 0.81 us -> 41.5 us  [shifted(): lax.ppermute(value, axis, [((i + distance) % size, i) for i in range(size)])]
    reduce_scatter x1 -> x0, waiting for transfers between devices: 28 us -> none  [layer(): lax.psum_scatter(jnp.dot(attn, w_out, preferred_element_type=jnp.float32)...]
    all_to_all x3 -> x6, starting transfers between devices: 28.3 us -> 40.7 us  [the longest x2 11.6 us: spread(): return lax.all_to_all(copies, axis, split_axis=0, concat_axis=0, tiled=True)]
    dot_general x8 -> x10, matrix products: 22.9 us -> 17 us  [the longest x4 13.2 us: per_device(): lax.dot_general(chunk, weight, (((1,), (1,)), ((), ())), preferred_elemen...]
    unnamed x27 -> x24, local copies, waits for them, and re-layouts: 0.57 us -> 5.1 us
    reduce_sum x5 -> x10, other arithmetic: 3.18 us -> 6.89 us  [the longest x4 4.55 us: per_device(): squares = squares + jnp.sum(wide * wide, axis=1)]
  transfers between devices with their start and end apart: 11 -> 12, of which waited for: 6 -> 9; matrix products, arithmetic and copies ran while one was open for 8% -> 23% of each run, Pallas kernels for 0% -> 0%
where the time goes in v1:
time: 184 us; the launch traced here: 183 us
  waiting for transfers between devices  79 us (43%)
  starting transfers between devices  46.7 us (25%)
  other arithmetic  22.6 us (12%)
  matrix products  17 us (9%)
  local copies, waits for them, and re-layouts  16.5 us (9%)
    ppermute x6, waiting for transfers between devices, shifted(): lax.ppermute(value, axis, [((i + distance) % size, i) for i in range(size)])  41.5 us
    dot_general x4, matrix products, per_device(): lax.dot_general(chunk, weight, (((1,), (1,)), ((), ())), preferred_elemen...  13.2 us
    all_to_all x1, waiting for transfers between devices, per_device(): lax.all_to_all(send, ALL, split_axis=0, concat_axis=0, tiled=True)  12.8 us
    all_to_all x2, starting transfers between devices, spread(): return lax.all_to_all(copies, axis, split_axis=0, concat_axis=0, tiled=True)  11.6 us
    all_to_all x1, starting transfers between devices, per_device(): lax.all_to_all(send, ALL, split_axis=0, concat_axis=0, tiled=True)  10.7 us
    all_to_all x2, waiting for transfers between devices, spread(): return lax.all_to_all(copies, axis, split_axis=0, concat_axis=0, tiled=True)  10.1 us
    all_to_all x1, starting transfers between devices, per_device(): got_v = lax.all_to_all(send_v, REP, split_axis=0, concat_axis=0, tiled=True)  9.47 us
    all_to_all x1, waiting for transfers between devices, per_device(): got_v = lax.all_to_all(send_v, REP, split_axis=0, concat_axis=0, tiled=True)  8.51 us
  transfers between devices with their start and end apart: 12, of which 9 were waited for; matrix products, arithmetic and copies ran while one was open for 23% of the time, Pallas kernels for 0%

profile of v1, /device:TPU:1, one launch (start us, length us, event | category | flops | bytes accessed | tf_op | source)
XLA Modules:
  0.0 183.0 jit_solution(11652920558776542574)
XLA Ops:
  1.6 1.1 fusion.21
  3.4 2.1 %convolution_add_fusion.2 = f32[32,256]{1,0:T(8,128)S(1)} fusion(bf16[3584,256]{1,0:T(8,128)(2,1)} %param.20, f32[256]{0:T(256)S(1)} %convert_element_type.111, bf16[32,3584]{1,0:T(8,128)(2,1)} %param.15, f32[3584]{0:T(1024)S(1)} %convert_element_type.109, f32[32]{0:T(128)S(1)} %add_rsqrt_fusion), kind=kOutput, calls=%fused_computation.30 | convolution fusion | flops 59187200 | bytes 2112640 | tf_op jit(solution)/shard_map/dot_general | solution.py:88
  7.5 3.3 %collective-permute-start = (bf16[32,384]{1,0:T(8,128)(2,1)S(1)}, bf16[32,384]{1,0:T(8,128)(2,1)S(1)}, u32[]{:S(2)}, u32[]{:S(2)}) collective-permute-start(bf16[32,384]{1,0:T(8,128)(2,1)S(1)} %pad_maximum_fusion.2), channel_id=1, source_target_pairs={{1,0},{0,1},{3,2},{2,3},{5,4},{4,5},{7,6},{6,7},{9,8},{8,9},{11,10... | collective-permute-start | bytes 73736 | tf_op jit(solution)/shard_map/ppermute | solution.py:13
  10.8 5.0 %multiply_convert_fusion = bf16[594,3584]{1,0:T(8,128)(2,1)} fusion(bf16[594,3584]{1,0:T(8,128)(2,1)} %param.29, f32[3584]{0:T(1024)S(1)} %convert_element_type.129), kind=kLoop, calls=%fused_computation.10 | loop fusion | flops 6386688 | bytes 8529920 | tf_op jit(solution)/shard_map/convert_element_type | solution.py:64
  21.1 2.6 %collective-permute-done.1 = f32[32,2,384]{0,1,2:T(2,128)S(1)} collective-permute-done((f32[32,2,384]{0,1,2:T(2,128)S(1)}, f32[32,2,384]{0,1,2:T(2,128)S(1)}, u32[]{:S(2)}, u32[]{:S(2)}) %collective-permute-start.1) | collective-permute-done | bytes 98336 | tf_op jit(solution)/shard_map/ppermute | solution.py:13
  25.0 3.4 %all-to-all-start = ((bf16[8,16,896]{2,1,0:T(8,128)(2,1)}), bf16[8,16,896]{2,1,0:T(8,128)(2,1)S(1)}, u32[]{:S(2)}, u32[]{:S(2)}) async-start(bf16[8,16,896]{2,1,0:T(8,128)(2,1)} %bitcast.6), calls=%async_computation | async-start | bytes 458752 | tf_op jit(solution)/shard_map/all_to_all | solution.py:155
  28.5 6.2 %all-to-all-done = bf16[8,16,896]{2,1,0:T(8,128)(2,1)S(1)} async-done(((bf16[8,16,896]{2,1,0:T(8,128)(2,1)}), bf16[8,16,896]{2,1,0:T(8,128)(2,1)S(1)}, u32[]{:S(2)}, u32[]{:S(2)}) %all-to-all-start) | async-done | bytes 229408 | tf_op jit(solution)/shard_map/all_to_all | solution.py:155
  35.5 7.6 %all-to-all-start.1 = ((bf16[8,16,896]{2,1,0:T(8,128)(2,1)}), bf16[8,16,896]{2,1,0:T(8,128)(2,1)S(1)}, u32[]{:S(2)}, u32[]{:S(2)}) async-start(bf16[8,16,896]{2,1,0:T(8,128)(2,1)} %broadcast_in_dim.169), calls=%async_computation.1 | async-start | bytes 458752 | tf_op jit(solution)/shard_map/all_to_all | solution.py:19
  43.3 9.2 %all-to-all-done.1 = bf16[8,16,896]{2,1,0:T(8,128)(2,1)S(1)} async-done(((bf16[8,16,896]{2,1,0:T(8,128)(2,1)}), bf16[8,16,896]{2,1,0:T(8,128)(2,1)S(1)}, u32[]{:S(2)}, u32[]{:S(2)}) %all-to-all-start.1) | async-done | bytes 229408 | tf_op jit(solution)/shard_map/all_to_all | solution.py:19
  53.6 4.0 %all-to-all-start.2 = ((bf16[4,128,896]{2,1,0:T(8,128)(2,1)}), bf16[4,128,896]{2,1,0:T(8,128)(2,1)S(1)}, u32[]{:S(2)}, u32[]{:S(2)}) async-start(bf16[4,128,896]{2,1,0:T(8,128)(2,1)} %broadcast_in_dim.171), calls=%async_computation.2 | async-start | bytes 1835008 | tf_op jit(solution)/shard_map/all_to_all | solution.py:19
  57.6 2.2 %bitcast_select_fusion = (bf16[32,64,128]{2,1,0:T(8,128)(2,1)S(1)}, bf16[32,64,128]{2,1,0:T(8,128)(2,1)}) fusion(bf16[32,1,64,128]{3,2,1,0:T(8,128)(2,1)} %param.17, pred[32,64]{1,0:T(8,128)(4,1)S(1)} %get-tuple-element.37, bf16[32,128]{1,0:T(8,128)(2,1)S(1)} %get-tuple-element.11, bf16[32,1,64,128]{3,2,1,0:T(8,128)(2,1)} %param.16, ...), kind=kLoop, calls=%fused_computation.39 | loop fusion | flops 524288 | bytes 2115584 | tf_op jit(solution)/shard_map/jit(_where)/select_n | solution.py:191
  59.8 2.7 %gather_fusion = bf16[64,64,128]{2,1,0:T(8,128)(2,1)} fusion(bf16[32,64,128]{2,1,0:T(8,128)(2,1)} %get-tuple-element.36, s32[1024]{0:T(1024)S(1)} %pad_clamp_fusion), kind=kCustom, calls=%fused_computation | custom fusion | bytes 2097408 | tf_op jit(solution)/shard_map/gather | solution.py:195
  62.5 1.6 gather_fusion.1
  64.1 3.1 %broadcast_select_fusion = (bf16[64,64,128]{2,1,0:T(8,128)(2,1)}, bf16[64,64,128]{2,1,0:T(8,128)(2,1)}) fusion(bf16[64,64,128]{2,1,0:T(8,128)(2,1)} %gather_fusion.1, pred[64]{0:T(512)(128)(4,1)S(1)} %fusion.35, bf16[64,64,128]{2,1,0:T(8,128)(2,1)} %gather_fusion), kind=kLoop, calls=%fused_computation.35 | loop fusion | flops 1048576 | bytes 4194368 | tf_op jit(solution)/shard_map/jit(_where)/select_n | solution.py:196
  68.0 5.5 %all-to-all-start.4 = ((bf16[64,64,128]{2,1,0:T(8,128)(2,1)}), bf16[64,64,128]{2,1,0:T(8,128)(2,1)}, u32[]{:S(2)}, u32[]{:S(2)}) async-start(bf16[64,64,128]{2,1,0:T(8,128)(2,1)} %get-tuple-element.42), calls=%async_computation.4 | async-start | bytes 2097152 | tf_op jit(solution)/shard_map/all_to_all | solution.py:197
  74.5 1.2 collective-permute-start.4
  76.1 16.1 %collective-permute-done.3 = bf16[512,896]{1,0:T(8,128)(2,1)} collective-permute-done((bf16[512,896]{1,0:T(8,128)(2,1)S(1)}, bf16[512,896]{1,0:T(8,128)(2,1)}, u32[]{:S(2)}, u32[]{:S(2)}) %collective-permute-start.3) | collective-permute-done | bytes 917536 | tf_op jit(solution)/shard_map/ppermute | solution.py:13
  92.1 1.4 multiply_reduce_fusion.2
  94.3 1.4 multiply_reduce_fusion.1
  95.8 22.2 %collective-permute-done.5 = bf16[512,896]{1,0:T(8,128)(2,1)} collective-permute-done((bf16[512,896]{1,0:T(8,128)(2,1)S(1)}, bf16[512,896]{1,0:T(8,128)(2,1)}, u32[]{:S(2)}, u32[]{:S(2)}) %collective-permute-start.5) | collective-permute-done | bytes 917536 | tf_op jit(solution)/shard_map/ppermute | solution.py:13
  118.0 1.4 multiply_reduce_fusion
  119.6 9.5 %all-to-all-start.5 = ((bf16[64,64,128]{2,1,0:T(8,128)(2,1)}), bf16[64,64,128]{2,1,0:T(8,128)(2,1)}, u32[]{:S(2)}, u32[]{:S(2)}) async-start(bf16[64,64,128]{2,1,0:T(8,128)(2,1)} %get-tuple-element.41), calls=%async_computation.5 | async-start | bytes 2097152 | tf_op jit(solution)/shard_map/all_to_all | solution.py:198
  129.0 3.3 %fusion.8 = f32[512,1188]{0,1:T(8,128)S(1)} fusion(bf16[512,896]{1,0:T(8,128)(2,1)} %collective-permute-done.3, s32[]{:T(128)S(6)} %select_n.164, bf16[594,3584]{1,0:T(8,128)(2,1)} %multiply_convert_fusion, bf16[594,3584]{1,0:T(8,128)(2,1)} %collective-permute-done.2), kind=kOutput, calls=%fused_computation.19 | convolution fusion | flops 1094252544 | bytes 11866116 | tf_op jit(solution)/shard_map/dot_general | solution.py:165
  132.4 3.3 %fusion.11 = f32[512,1188]{0,1:T(8,128)S(1)} fusion(bf16[512,896]{1,0:T(8,128)(2,1)} %collective-permute-done.4, s32[]{:T(128)S(6)} %select_n.166, bf16[594,3584]{1,0:T(8,128)(2,1)} %multiply_convert_fusion, bf16[594,3584]{1,0:T(8,128)(2,1)} %collective-permute-done.2), kind=kOutput, calls=%fused_computation.21 | convolution fusion | flops 1094252544 | bytes 11866116 | tf_op jit(solution)/shard_map/dot_general | solution.py:165
  135.7 3.3 %fusion.3 = f32[512,1188]{0,1:T(8,128)S(1)} fusion(bf16[512,896]{1,0:T(8,128)(2,1)} %collective-permute-done.5, s32[]{:T(128)S(6)} %select_n.168, bf16[594,3584]{1,0:T(8,128)(2,1)} %multiply_convert_fusion, bf16[594,3584]{1,0:T(8,128)(2,1)} %collective-permute-done.2), kind=kOutput, calls=%fused_computation.16 | convolution fusion | flops 1094252544 | bytes 11866116 | tf_op jit(solution)/shard_map/dot_general | solution.py:165
  139.0 3.2 %fusion.13 = f32[512]{0:T(512)S(1)} fusion(f32[512,1188]{0,1:T(8,128)S(1)} %fusion.3, f32[512,1188]{0,1:T(8,128)S(1)} %fusion.11, f32[512,1188]{0,1:T(8,128)S(1)} %fusion.8, bf16[512,896]{1,0:T(8,128)(2,1)S(1)} %bitcast.59, s32[]{:T(128)S(6)} %select_n.162, bf16[594,3584]{1,0:T(8,128)(2,1)} %multiply_convert_fusion, ...), kind=kOutput, calls=%fused_computation.26 | convolution fusion | flops 1096685056 | bytes 16734212 | tf_op jit(solution)/shard_map/dot_general | solution.py:165
  143.5 1.9 %all_to_all.24 = f32[256,1,16]{2,0,1:T(8,128)} reshape(f32[32,32,2,2]{3,2,1,0:T(2,128)S(1)} %copy.97) | data formatting | bytes 32768 | tf_op jit(solution)/shard_map/all_to_all | solution.py:181
  145.4 8.5 %all-to-all-done.5 = bf16[64,64,128]{2,1,0:T(8,128)(2,1)} async-done(((bf16[64,64,128]{2,1,0:T(8,128)(2,1)}), bf16[64,64,128]{2,1,0:T(8,128)(2,1)}, u32[]{:S(2)}, u32[]{:S(2)}) %all-to-all-start.5) | async-done | bytes 1048608 | tf_op jit(solution)/shard_map/all_to_all | solution.py:198
  153.9 10.7 %all-to-all-start.3 = ((f32[256,1,16]{2,1,0:T(1,128)}), f32[256,1,16]{2,1,0:T(1,128)S(1)}, u32[]{:S(2)}, u32[]{:S(2)}) async-start(f32[256,1,16]{2,1,0:T(1,128)} %bitcast.12), calls=%async_computation.3 | async-start | bytes 262144 | tf_op jit(solution)/shard_map/all_to_all | solution.py:181
  164.6 12.8 %all-to-all-done.3 = f32[256,1,16]{2,1,0:T(1,128)S(1)} async-done(((f32[256,1,16]{2,1,0:T(1,128)}), f32[256,1,16]{2,1,0:T(1,128)S(1)}, u32[]{:S(2)}, u32[]{:S(2)}) %all-to-all-start.3) | async-done | bytes 16416 | tf_op jit(solution)/shard_map/all_to_all | solution.py:181
  178.5 2.3 %copy.109 = bf16[64,1,64,128]{3,2,1,0:T(8,128)(2,1)} copy(bf16[64,1,64,128]{3,2,1,0:T(8,128)(2,1)} %bitcast.16) | data formatting | bytes 2097152
  180.8 2.3 %copy.110 = bf16[64,1,64,128]{3,2,1,0:T(8,128)(2,1)} copy(bf16[64,1,64,128]{3,2,1,0:T(8,128)(2,1)} %bitcast.17) | data formatting | bytes 2097152
  (114 shorter events, 17.5 us)
Async XLA Ops:
  0.6 23.2 %copy-start = (bf16[256,3584]{1,0:T(8,128)(2,1)S(1)}, bf16[256,3584]{1,0:T(8,128)(2,1)}, u32[]{:S(2)}) copy-start(bf16[256,3584]{1,0:T(8,128)(2,1)} %param.26) | copy-start | bytes 5505028
  0.6 6.1 %copy-start.2 = (bf16[32,3584]{1,0:T(8,128)(2,1)S(1)}, bf16[32,3584]{1,0:T(8,128)(2,1)}, u32[]{:S(2)}) copy-start(bf16[32,3584]{1,0:T(8,128)(2,1)} %param.15) | copy-start | bytes 688132
  0.7 6.0 %copy-start.8 = (bf16[64]{0:T(256)(128)(2,1)S(1)}, bf16[64]{0:T(256)(128)(2,1)}, u32[]{:S(2)}) copy-start(bf16[64]{0:T(256)(128)(2,1)} %param.23) | copy-start | bytes 388
  0.7 6.0 %copy-start.9 = (bf16[64]{0:T(256)(128)(2,1)S(1)}, bf16[64]{0:T(256)(128)(2,1)}, u32[]{:S(2)}) copy-start(bf16[64]{0:T(256)(128)(2,1)} %param.25) | copy-start | bytes 388
  0.7 6.1 %copy-start.6 = (bf16[3584,64]{0,1:T(8,128)(2,1)S(1)}, bf16[3584,64]{0,1:T(8,128)(2,1)}, u32[]{:S(2)}) copy-start(bf16[3584,64]{0,1:T(8,128)(2,1)} %param.22) | copy-start | bytes 1376260
  0.7 6.4 %copy-start.7 = (bf16[3584,64]{0,1:T(8,128)(2,1)S(1)}, bf16[3584,64]{0,1:T(8,128)(2,1)}, u32[]{:S(2)}) copy-start(bf16[3584,64]{0,1:T(8,128)(2,1)} %param.24) | copy-start | bytes 1376260
  0.7 10.0 %copy-start.4 = (bf16[3584]{0:T(1024)(128)(2,1)S(1)}, bf16[3584]{0:T(1024)(128)(2,1)}, u32[]{:S(2)}) copy-start(bf16[3584]{0:T(1024)(128)(2,1)} %param.28) | copy-start | bytes 21508
  7.5 9.7 %collective-permute-start = (bf16[32,384]{1,0:T(8,128)(2,1)S(1)}, bf16[32,384]{1,0:T(8,128)(2,1)S(1)}, u32[]{:S(2)}, u32[]{:S(2)}) collective-permute-start(bf16[32,384]{1,0:T(8,128)(2,1)S(1)} %pad_maximum_fusion.2), channel_id=1, source_target_pairs={{1,0},{0,1},{3,2},{2,3},{5,4},{4,5},{7,6},{6,7},{9,8},{8,9},{11,10... | collective-permute-start | bytes 73736 | tf_op jit(solution)/shard_map/ppermute | solution.py:13
  10.7 5.7 %copy-start.5 = (s32[1024,1]{0,1:T(1,128)S(1)}, s32[1024,1]{0,1:T(1,128)}, u32[]{:S(2)}) copy-start(s32[1024,1]{0,1:T(1,128)} %param.19) | copy-start | bytes 12292
  10.7 7.0 %copy-start.1 = (bf16[32,1,64,128]{3,2,1,0:T(8,128)(2,1)S(1)}, bf16[32,1,64,128]{3,2,1,0:T(8,128)(2,1)}, u32[]{:S(2)}) copy-start(bf16[32,1,64,128]{3,2,1,0:T(8,128)(2,1)} %param.16) | copy-start | bytes 1572868
  10.7 7.9 %copy-start.3 = (bf16[32,1,64,128]{3,2,1,0:T(8,128)(2,1)S(1)}, bf16[32,1,64,128]{3,2,1,0:T(8,128)(2,1)}, u32[]{:S(2)}) copy-start(bf16[32,1,64,128]{3,2,1,0:T(8,128)(2,1)} %param.17) | copy-start | bytes 1572868
  15.7 113.3 %collective-permute-start.2 = (bf16[594,3584]{1,0:T(8,128)(2,1)}, bf16[594,3584]{1,0:T(8,128)(2,1)}, u32[]{:S(2)}, u32[]{:S(2)}) collective-permute-start(bf16[594,3584]{1,0:T(8,128)(2,1)} %multiply_convert_fusion), channel_id=1, source_target_pairs={{1,0},{0,1},{3,2},{2,3},{5,4},{4,5},{7,6},{6,7},{9,8},{8,9},{11,10... | collective-permute-start | bytes 12773384 | tf_op jit(solution)/shard_map/ppermute | solution.py:13
  19.7 3.9 %collective-permute-start.1 = (f32[32,2,384]{0,1,2:T(2,128)S(1)}, f32[32,2,384]{0,1,2:T(2,128)S(1)}, u32[]{:S(2)}, u32[]{:S(2)}) collective-permute-start(f32[32,2,384]{0,1,2:T(2,128)S(1)} %bitcast.65), channel_id=1, source_target_pairs={{1,0},{0,1},{3,2},{2,3},{5,4},{4,5},{7,6},{6,7},{9,8},{8,9},{11,10... | collective-permute-start | bytes 294920 | tf_op jit(solution)/shard_map/ppermute | solution.py:13
  25.0 9.7 %all-to-all-start = ((bf16[8,16,896]{2,1,0:T(8,128)(2,1)}), bf16[8,16,896]{2,1,0:T(8,128)(2,1)S(1)}, u32[]{:S(2)}, u32[]{:S(2)}) async-start(bf16[8,16,896]{2,1,0:T(8,128)(2,1)} %bitcast.6), calls=%async_computation | async-start | bytes 458752 | tf_op jit(solution)/shard_map/all_to_all | solution.py:155
  35.5 17.0 %all-to-all-start.1 = ((bf16[8,16,896]{2,1,0:T(8,128)(2,1)}), bf16[8,16,896]{2,1,0:T(8,128)(2,1)S(1)}, u32[]{:S(2)}, u32[]{:S(2)}) async-start(bf16[8,16,896]{2,1,0:T(8,128)(2,1)} %broadcast_in_dim.169), calls=%async_computation.1 | async-start | bytes 458752 | tf_op jit(solution)/shard_map/all_to_all | solution.py:19
  53.6 14.4 %all-to-all-start.2 = ((bf16[4,128,896]{2,1,0:T(8,128)(2,1)}), bf16[4,128,896]{2,1,0:T(8,128)(2,1)S(1)}, u32[]{:S(2)}, u32[]{:S(2)}) async-start(bf16[4,128,896]{2,1,0:T(8,128)(2,1)} %broadcast_in_dim.171), calls=%async_computation.2 | async-start | bytes 1835008 | tf_op jit(solution)/shard_map/all_to_all | solution.py:19
  68.0 51.5 %all-to-all-start.4 = ((bf16[64,64,128]{2,1,0:T(8,128)(2,1)}), bf16[64,64,128]{2,1,0:T(8,128)(2,1)}, u32[]{:S(2)}, u32[]{:S(2)}) async-start(bf16[64,64,128]{2,1,0:T(8,128)(2,1)} %get-tuple-element.42), calls=%async_computation.4 | async-start | bytes 2097152 | tf_op jit(solution)/shard_map/all_to_all | solution.py:197
  73.5 18.6 %collective-permute-start.3 = (bf16[512,896]{1,0:T(8,128)(2,1)S(1)}, bf16[512,896]{1,0:T(8,128)(2,1)}, u32[]{:S(2)}, u32[]{:S(2)}) collective-permute-start(bf16[512,896]{1,0:T(8,128)(2,1)S(1)} %bitcast.56), channel_id=1, source_target_pairs={{2,0},{4,2},{6,4},{0,6},{3,1},{5,3},{7,5},{1,7},{10,8},{12,10},{14... | collective-permute-start | bytes 2752520 | tf_op jit(solution)/shard_map/ppermute | solution.py:13
  74.5 19.8 %collective-permute-start.4 = (bf16[512,896]{1,0:T(8,128)(2,1)S(1)}, bf16[512,896]{1,0:T(8,128)(2,1)}, u32[]{:S(2)}, u32[]{:S(2)}) collective-permute-start(bf16[512,896]{1,0:T(8,128)(2,1)S(1)} %bitcast.57), channel_id=1, source_target_pairs={{4,0},{6,2},{0,4},{2,6},{5,1},{7,3},{1,5},{3,7},{12,8},{14,10},{8,... | collective-permute-start | bytes 2752520 | tf_op jit(solution)/shard_map/ppermute | solution.py:13
  75.6 42.4 %collective-permute-start.5 = (bf16[512,896]{1,0:T(8,128)(2,1)S(1)}, bf16[512,896]{1,0:T(8,128)(2,1)}, u32[]{:S(2)}, u32[]{:S(2)}) collective-permute-start(bf16[512,896]{1,0:T(8,128)(2,1)S(1)} %bitcast.58), channel_id=1, source_target_pairs={{6,0},{0,2},{2,4},{4,6},{7,1},{1,3},{3,5},{5,7},{14,8},{8,10},{10,... | collective-permute-start | bytes 2752520 | tf_op jit(solution)/shard_map/ppermute | solution.py:13
  119.6 34.4 %all-to-all-start.5 = ((bf16[64,64,128]{2,1,0:T(8,128)(2,1)}), bf16[64,64,128]{2,1,0:T(8,128)(2,1)}, u32[]{:S(2)}, u32[]{:S(2)}) async-start(bf16[64,64,128]{2,1,0:T(8,128)(2,1)} %get-tuple-element.41), calls=%async_computation.5 | async-start | bytes 2097152 | tf_op jit(solution)/shard_map/all_to_all | solution.py:198
  153.9 23.5 %all-to-all-start.3 = ((f32[256,1,16]{2,1,0:T(1,128)}), f32[256,1,16]{2,1,0:T(1,128)S(1)}, u32[]{:S(2)}, u32[]{:S(2)}) async-start(f32[256,1,16]{2,1,0:T(1,128)} %bitcast.12), calls=%async_computation.3 | async-start | bytes 262144 | tf_op jit(solution)/shard_map/all_to_all | solution.py:181

commit v2 on v1

--- a/solution.py
+++ b/solution.py
@@ -1,11 +1,14 @@
 import jax
 import jax.numpy as jnp
 from jax import lax
+from jax.experimental import pallas as pl
+from jax.experimental.pallas import tpu as pltpu
 from jax.sharding import Mesh, PartitionSpec as P
 
 REP = ("x", "z")
 TP = ("y", "c")
 ALL = ("x", "z", "y", "c")
+HBM = pltpu.MemorySpace.HBM
 
 
 def shifted(value, axis, distance):
@@ -24,6 +27,228 @@
     first = vals[..., :half]
     second = vals[..., half:]
     return jnp.concatenate([first * cos - second * sin, second * cos + first * sin], axis=-1)
+
+
+def ring(block, axis):
+    size = lax.axis_size(axis)
+
+    def from_side(value, step):
+        pairs = [
+            (((i + (step if c == 0 else -step)) % size) * 2 + c, i * 2 + c)
+            for i in range(size)
+            for c in range(2)
+        ]
+        return lax.ppermute(value, (axis, "c"), pairs)
+
+    first = from_side(block, 1)
+    second = from_side(block, -1)
+    return [block, first, from_side(first, 1), second]
+
+
+def head_kernel(y_ref, *refs):
+    sources = refs[:8]
+    gain, row, lane, own, other, out, x, weights = refs[8:16]
+    landed = refs[16:24]
+    chunk_sems, weight_sems = refs[24:]
+    f32 = jnp.float32
+    bf16 = jnp.bfloat16
+    copies = [
+        pltpu.make_async_copy(source, target, chunk_sems.at[i])
+        for i, (source, target) in enumerate(zip(sources, landed))
+    ]
+    vocab, width = own.shape
+    split = vocab // 16 * 8
+    tiles = [(i, low, high) for i in range(2) for low, high in ((0, split), (split, vocab))]
+    loads = [
+        pltpu.make_async_copy(
+            (own, other)[i].at[low:high], weights.at[i, low:high], weight_sems.at[at]
+        )
+        for at, (i, low, high) in enumerate(tiles)
+    ]
+    for copy in copies:
+        copy.start()
+    n, quarter, cols = landed[0].shape
+    sums = [0.0] * (2 * n)
+    for copy in copies:
+        copy.wait()
+    for load in loads:
+        load.start()
+    for d in range(n):
+        start_a = pl.multiple_of(y_ref[1, d] * cols, 128)
+        start_b = pl.multiple_of(y_ref[0, d] * cols, 128)
+        scale_a = gain[:, pl.ds(start_a, cols)].astype(f32)
+        scale_b = gain[:, pl.ds(start_b, cols)].astype(f32)
+        for i in range(2 * n):
+            if i < n:
+                piece, start, scale = landed[d][i], start_a, scale_a
+            else:
+                piece, start, scale = landed[i][d], start_b, scale_b
+            wide = piece.astype(f32)
+            sums[i] = sums[i] + jnp.sum(wide * wide, axis=1, keepdims=True)
+            x[pl.ds(i * quarter, quarter), pl.ds(start, cols)] = (wide * scale).astype(bf16)
+    dims = (((1,), (1,)), ((), ()))
+    top = None
+    for load, (i, low, high) in zip(loads, tiles):
+        load.wait()
+        logits = lax.dot_general(weights[i, low:high, :], x[...], dims, preferred_element_type=f32)
+        peak = jnp.max(logits, axis=0, keepdims=True)
+        top = peak if top is None else jnp.maximum(top, peak)
+
+    ms = jnp.concatenate(sums, axis=0) / width
+    here = lax.broadcasted_iota(jnp.int32, (out.shape[0], row.shape[1]), 0) == row[...]
+    lanes = lax.broadcasted_iota(jnp.int32, (row.shape[1], out.shape[1]), 1)
+    at = lane[...]
+    place = (lanes == at).astype(f32)
+    rest = jnp.where(lanes == at + 8, ms, 0.0) + (lanes == at + 16).astype(f32)
+    exact = lax.Precision.HIGHEST
+    out[...] = jnp.dot(
+        jnp.where(here, top, 0.0), place, precision=exact, preferred_element_type=f32
+    ) + jnp.dot(here.astype(f32), rest, precision=exact, preferred_element_type=f32)
+
+
+def head(y_pos, chunks_a, chunks_b, gain, row, lane, own, other, targets):
+    chunks = chunks_a + chunks_b
+    vocab, width = own.shape
+    count = row.shape[1]
+    vmem = pl.BlockSpec(memory_space=pltpu.VMEM)
+    hbm = pl.BlockSpec(memory_space=HBM)
+    return pl.pallas_call(
+        head_kernel,
+        in_specs=[pl.BlockSpec(memory_space=pltpu.SMEM)]
+        + [hbm] * len(chunks)
+        + [vmem] * 3
+        + [hbm] * 2,
+        out_specs=vmem,
+        scratch_shapes=[
+            pltpu.VMEM((count, width), jnp.bfloat16),
+            pltpu.VMEM((2, vocab, width), jnp.bfloat16),
+        ]
+        + [pltpu.VMEM(value.shape, value.dtype) for value in chunks]
+        + [pltpu.SemaphoreType.DMA((len(chunks),)), pltpu.SemaphoreType.DMA((4,))],
+        out_shape=jax.ShapeDtypeStruct((targets, 128), jnp.float32),
+        compiler_params=pltpu.CompilerParams(vmem_limit_bytes=60 * 1024 * 1024),
+        name="head",
+    )(y_pos, *chunks, gain[None], row, lane, own, other)
+
+
+def after_kernel(value, other, out):
+    del other, out
+
+
+def after(value, *others):
+    hbm = pl.BlockSpec(memory_space=HBM)
+    for other in others:
+        value = pl.pallas_call(
+            after_kernel,
+            in_specs=[hbm, hbm],
+            out_specs=hbm,
+            out_shape=jax.ShapeDtypeStruct(value.shape, value.dtype),
+            input_output_aliases={0: 0},
+            name="after",
+        )(value, other)
+    return value
+
+
+def project_kernel(x_ref, gain, bias, cos, sin, wq_ref, wk_ref, wv_ref, out, wq, wk, wv, sems):
+    f32 = jnp.float32
+    bf16 = jnp.bfloat16
+    loads = [
+        pltpu.make_async_copy(source, target, sems.at[i])
+        for i, (source, target) in enumerate(((wq_ref, wq), (wk_ref, wk), (wv_ref, wv)))
+    ]
+    for load in loads:
+        load.start()
+    x = x_ref[...].astype(f32)
+    mean = jnp.mean(x * x, axis=1, keepdims=True)
+    normed = (x * lax.rsqrt(mean + 1e-06) * gain[...].astype(f32)).astype(bf16)
+    for load in loads:
+        load.wait()
+    query = jnp.dot(normed, wq[...], preferred_element_type=f32)
+    dims = (((1,), (1,)), ((), ()))
+    rest = [
+        lax.dot_general(normed, weight[...], dims, preferred_element_type=f32)
+        for weight in (wk, wv)
+    ]
+    c, s = cos[...], sin[...]
+    half = c.shape[1]
+    at = query.shape[1]
+    query = query + bias[:, :at].astype(f32)
+    for low in range(0, at, 2 * half):
+        first = query[:, low : low + half]
+        second = query[:, low + half : low + 2 * half]
+        out[:, low : low + 2 * half] = jnp.concatenate(
+            [first * c - second * s, second * c + first * s], axis=1
+        ).astype(bf16)
+    out[:, at:] = (jnp.concatenate(rest, axis=1) + bias[:, at:].astype(f32)).astype(bf16)
+
+
+def project(x, gain, wq, bq, wk, bk, wv, bv, cos, sin):
+    width = wq.shape[1] + wk.shape[1] + wv.shape[1]
+    vmem = pl.BlockSpec(memory_space=pltpu.VMEM)
+    hbm = pl.BlockSpec(memory_space=HBM)
+    weights = (wq, wk.T, wv.T)
+    return pl.pallas_call(
+        project_kernel,
+        in_specs=[vmem] * 5 + [hbm] * 3,
+        out_specs=vmem,
+        out_shape=jax.ShapeDtypeStruct((x.shape[0], width), jnp.bfloat16),
+        scratch_shapes=[pltpu.VMEM(w.shape, w.dtype) for w in weights]
+        + [pltpu.SemaphoreType.DMA((3,))],
+        compiler_params=pltpu.CompilerParams(vmem_limit_bytes=60 * 1024 * 1024),
+        name="project",
+    )(x, gain[None], jnp.concatenate([bq, bk, bv])[None], cos, sin, *weights)
+
+
+def pack_kernel(pick, at, keys, values, key_new, value_new, out):
+    half = keys.shape[2]
+    place = lax.broadcasted_iota(jnp.int32, (half, keys.shape[3]), 0)
+
+    def body(slot, carry):
+        source = pick[slot]
+        from_row = jnp.maximum(source, 0)
+        live = jnp.broadcast_to(source, place.shape) >= 0
+        written = place == at[from_row]
+        for i, (cache, new) in enumerate(((keys, key_new), (values, value_new))):
+            old = cache[from_row, 0].astype(jnp.float32)
+            full = jnp.where(written, new[pl.ds(from_row, 1), :], old)
+            out[slot, i * half : (i + 1) * half, :] = jnp.where(live, full, 0.0).astype(out.dtype)
+        return carry
+
+    lax.fori_loop(0, out.shape[0], body, 0, unroll=4)
+
+
+def pack(pick, at, keys, values, key_new, value_new):
+    _, _, half, head_size = keys.shape
+    smem = pl.BlockSpec(memory_space=pltpu.SMEM)
+    vmem = pl.BlockSpec(memory_space=pltpu.VMEM)
+    return pl.pallas_call(
+        pack_kernel,
+        in_specs=[smem] * 2 + [vmem] * 4,
+        out_specs=vmem,
+        out_shape=jax.ShapeDtypeStruct((pick.shape[0], 2 * half, head_size), keys.dtype),
+        compiler_params=pltpu.CompilerParams(vmem_limit_bytes=60 * 1024 * 1024),
+        name="pack",
+    )(pick, at, keys, values, key_new, value_new)
+
+
+def settle_kernel(got, keys, values):
+    half = keys.shape[2]
+    keys[:, 0] = got[:, :half]
+    values[:, 0] = got[:, half:]
+
+
+def settle(got):
+    serve, length, head_size = got.shape
+    step = serve // 8
+    shape = jax.ShapeDtypeStruct((serve, 1, length // 2, head_size), got.dtype)
+    return pl.pallas_call(
+        settle_kernel,
+        grid=(8,),
+        in_specs=[pl.BlockSpec((step, length, head_size), lambda i: (i, 0, 0))],
+        out_specs=[pl.BlockSpec((step, 1, length // 2, head_size), lambda i: (i, 0, 0, 0))] * 2,
+        out_shape=[shape, shape],
+        name="settle",
+    )(got)
 
 
 def per_device(
@@ -61,11 +286,7 @@
     cols = width // n_y
     rows = slots // 2
 
-    scaled = (w_head.astype(f32) * gain_out.astype(f32)[None, :]).astype(bf16)
-    head = jnp.concatenate([scaled, shifted(scaled, "c", 1)], axis=0)
-    head_parts = [
-        lax.dynamic_slice_in_dim(head, ((y_pos + d) % n_y) * cols, cols, 1) for d in range(n_y)
-    ]
+    head_other = shifted(w_head, "c", 1)
 
     flat = routes[:, 0].reshape(n_rep, slots)
     earlier = (flat[:, None, :] == flat[:, :, None]) & (
@@ -76,30 +297,18 @@
     own_bucket = lax.dynamic_slice_in_dim(bucket, rep_pos, 1, 0)[0]
     lens = lax.dynamic_slice_in_dim(lengths, rep_pos * slots, slots, 0)
 
-    xf = hidden_in.astype(f32)
-    normed_in = (
-        xf * lax.rsqrt(jnp.mean(xf * xf, axis=1, keepdims=True) + eps) * gain_in.astype(f32)
-    ).astype(bf16)
     half = head_size // 2
     freq = 1000000.0 ** (-(jnp.arange(half, dtype=f32) * 2.0 / head_size))
     angle = lens.astype(f32)[:, None] * freq
     cos, sin = jnp.cos(angle), jnp.sin(angle)
-    query = (
-        jnp.dot(normed_in, w_query, preferred_element_type=f32) + b_query.astype(f32)
-    ).reshape(slots, -1, head_size)
-    query = rotate(query, cos[:, None], sin[:, None]).astype(bf16)
-    key_part = (jnp.dot(normed_in, w_key, preferred_element_type=f32) + b_key.astype(f32)).astype(
-        bf16
-    )
-    value_part = (
-        jnp.dot(normed_in, w_value, preferred_element_type=f32) + b_value.astype(f32)
-    ).astype(bf16)
-    packed = jnp.concatenate([query.reshape(slots, -1), key_part, value_part], axis=1)
+    packed = project(
+        hidden_in, gain_in, w_query, b_query, w_key, b_key, w_value, b_value, cos, sin
+    )
     other = shifted(packed, "c", 1)
     first = jnp.where(even, packed, other)
     second = jnp.where(even, other, packed)
-    q_width = query.shape[1] * head_size
-    k_width = key_part.shape[1]
+    q_width = w_query.shape[1]
+    k_width = w_key.shape[1]
     queries = jnp.concatenate([first[:, :q_width], second[:, :q_width]], axis=1).reshape(
         slots, -1, head_size
     )
@@ -150,53 +359,65 @@
     )
     attn = merged.reshape(slots, -1).astype(bf16)
 
+    hits = own_bucket[None, :] == jnp.arange(serve, dtype=jnp.int32)[:, None]
+    pick = jnp.max(jnp.where(hits, jnp.arange(slots, dtype=jnp.int32)[None, :], -1), axis=1)
+    send_kv = pack(
+        pick, lens - c_pos * half_len, k_cache, v_cache, key_new.astype(f32), value_new.astype(f32)
+    )
+
     partial = jnp.dot(attn, w_out, preferred_element_type=f32).astype(bf16)
     partial = partial.reshape(2, rows, n_y, cols).transpose(2, 0, 1, 3).reshape(n_tp, rows, cols)
     shares = lax.all_to_all(partial, TP, split_axis=0, concat_axis=0, tiled=True)
     own_x = lax.dynamic_slice(hidden_in, (c_pos * rows, y_pos * cols), (rows, cols))
     state = (own_x.astype(f32) + jnp.sum(shares.astype(f32), axis=0)).astype(bf16)
 
-    gathered = spread(state, "z").reshape(n_z * rows, cols)
-    gathered = spread(gathered, "x").reshape(n_rep * rows, cols)
-    chunks = [gathered] + [shifted(gathered, "y", d) for d in range(1, n_y)]
-    logits = 0.0
-    squares = 0.0
-    for chunk, weight in zip(chunks, head_parts):
-        logits = logits + lax.dot_general(
-            chunk, weight, (((1,), (1,)), ((), ())), preferred_element_type=f32
-        )
-        wide = chunk.astype(f32)
-        squares = squares + jnp.sum(wide * wide, axis=1)
-    ms = squares / width
-    best = (jnp.max(logits, axis=1) * lax.rsqrt(ms + eps)).reshape(n_rep, 1, rows)
-    rms = jnp.sqrt(ms).reshape(n_rep, 1, rows)
-
+    n_x = lax.axis_size("x")
+    part = rows // 2
+    by_z = spread(state, "z")
+    part_a = by_z[:, :part].reshape(n_z * part, cols)
+    part_b = by_z[:, part:].reshape(n_z * part, cols)
+    from_x = [part_a] + [shifted(part_a, "x", d) for d in range(1, n_x)]
+    from_y = [part_b] + [shifted(part_b, "y", d) for d in range(1, n_y)]
+    by_z = after(by_z, send_kv)
+    block_a = jnp.stack(from_x)
+    block_b = jnp.stack(from_y)
+    chunks_a = ring(block_a, "y")
+    chunks_b = ring(block_b, "x")
     own_rows = lax.dynamic_slice(bucket, (0, c_pos * rows), (n_rep, rows))
-    hit = own_rows[:, None, :] == jnp.arange(serve, dtype=jnp.int32)[None, :, None]
-    send_best = jnp.max(jnp.where(hit, best, -jnp.inf), axis=2)
-    send_rms = jnp.max(jnp.where(hit, rms, -1.0), axis=2)
-    send = jnp.stack([send_best, send_rms], axis=0).reshape(2, n_rep, n_rep, cap)
-    send = send.transpose(2, 1, 0, 3).reshape(n_rep, n_tp, n_rep // n_tp, 2, cap)
-    send = send.reshape(n_rep * n_tp, -1)
-    arrived = jnp.max(lax.all_to_all(send, ALL, split_axis=0, concat_axis=0, tiled=True), axis=0)
-    arrived = arrived.reshape(n_rep // n_tp, 2, cap)
-    arrived_best = arrived[:, 0].reshape(-1)
-    arrived_rms = arrived[:, 1].reshape(-1)
-    taken = arrived_rms >= 0.0
-    final_norm = jnp.where(taken, arrived_rms, 0.0)
-    top_logit = jnp.where(taken, arrived_best, 0.0)
-
-    written = (place[None, :] == lens[:, None])[:, :, None]
-    keys_full = jnp.where(written, key_new[:, None, :], keys)
-    values_full = jnp.where(written, value_new[:, None, :], values)
-    hits = own_bucket[None, :] == jnp.arange(serve, dtype=jnp.int32)[:, None]
-    pick = jnp.sum(jnp.where(hits, jnp.arange(slots, dtype=jnp.int32)[None, :], 0), axis=1)
-    filled = jnp.any(hits, axis=1)[:, None, None]
-    send_k = jnp.where(filled, keys_full[pick], jnp.zeros((), bf16))
-    send_v = jnp.where(filled, values_full[pick], jnp.zeros((), bf16))
-    got_k = lax.all_to_all(send_k, REP, split_axis=0, concat_axis=0, tiled=True)
-    got_v = lax.all_to_all(send_v, REP, split_axis=0, concat_axis=0, tiled=True)
-    return (final_norm, top_logit, got_k[:, None], got_v[:, None])
+    source = jnp.arange(n_rep, dtype=jnp.int32)[:, None]
+    per_tp = n_rep // n_tp
+    row = own_rows // cap * n_tp + source // per_tp
+    lane = source % per_tp * cap + own_rows % cap
+
+    def in_chunk_order(table):
+        table = table.reshape(n_x, n_z, 2, part).transpose(2, 0, 1, 3)
+        table = jnp.roll(table, -lax.axis_index("x"), axis=1)
+        mirrored = jnp.concatenate([table[:, :1], table[:, :0:-1]], axis=1)
+        return jnp.stack([table[0], jnp.where(even, table[1], mirrored[1])])
+
+    steps = jnp.arange(n_y, dtype=jnp.int32)
+    y_of_chunk = jnp.stack(
+        [(y_pos + steps) % n_y, (y_pos + jnp.where(even, steps, n_y - steps)) % n_y]
+    )
+
+    row = in_chunk_order(row).reshape(1, -1)
+    lane = in_chunk_order(lane).reshape(-1, 1)
+    send = head(
+        y_of_chunk, chunks_a, chunks_b, gain_out, row, lane, w_head, head_other, n_rep * n_tp
+    )
+    got = lax.all_to_all(send_kv, REP, split_axis=0, concat_axis=0, tiled=True)
+    keys_out, values_out = settle(got)
+    send = after(send, got)[:, None]
+    arrived = lax.all_to_all(send, ALL, split_axis=0, concat_axis=0, tiled=True)
+    arrived = after(arrived, keys_out)[:, 0]
+    slots_here = per_tp * cap
+    present = arrived[:, 2 * slots_here : 3 * slots_here] > 0.0
+    best = jnp.max(jnp.where(present, arrived[:, :slots_here], -jnp.inf), axis=0)
+    ms = jnp.max(arrived[:, slots_here : 2 * slots_here], axis=0)
+    taken = jnp.any(present, axis=0)
+    final_norm = jnp.where(taken, jnp.sqrt(ms), 0.0)
+    top_logit = jnp.where(taken, best * lax.rsqrt(ms + eps), 0.0)
+    return (final_norm, top_logit, keys_out, values_out)
 
 
 def solution(mesh):

time: 184 us -> 143 us (0.78)
  waiting for transfers between devices: 79 us -> 44.7 us
  Pallas kernels: 0 us -> 26.1 us
  matrix products: 17 us -> 1.18 us
  other arithmetic: 22.6 us -> 10.2 us
  local copies, waits for them, and re-layouts: 16.5 us -> 8.51 us
  starting transfers between devices: 46.7 us -> 49.8 us
    ppermute x6 -> x9, waiting for transfers between devices: 41.5 us -> 10.3 us  [shifted(): lax.ppermute(value, axis, [((i + distance) % size, i) for i in range(size)])]
    pallas_call x0 -> x6, Pallas kernels: none -> 26.1 us  [the longest x1 13.1 us: head(): pl.pallas_call(head_kernel, in_specs=[pl.BlockSpec(memory_space=pltpu.SME...]
    ppermute x0 -> x6, waiting for transfers between devices: none -> 18 us  [from_side(): return lax.ppermute(value, (axis, 'c'), pairs)]
    dot_general x7 -> x0, matrix products: 15.9 us -> none  [the longest x4 13.2 us: per_device(): lax.dot_general(chunk, weight, (((1,), (1,)), ((), ())), preferred_elemen...]
    all_to_all x3 -> x2, waiting for transfers between devices: 21.3 us -> 7.21 us  [the longest x1 7.21 us: per_device(): arrived = lax.all_to_all(send, ALL, split_axis=0, concat_axis=0, tiled=True)]
    ppermute x0 -> x6, starting transfers between devices: none -> 10.2 us  [from_side(): return lax.ppermute(value, (axis, 'c'), pairs)]
    all_to_all x3 -> x2, starting transfers between devices: 25.6 us -> 17.3 us  [the longest x1 11.7 us: per_device(): arrived = lax.all_to_all(send, ALL, split_axis=0, concat_axis=0, tiled=True)]
    convert_element_type x6 -> x0, other arithmetic: 6.52 us -> none  [the longest x2 4.99 us: per_device(): scaled = (w_head.astype(f32) * gain_out.astype(f32)[None, :]).astype(bf16)]
  transfers between devices with their start and end apart: 12 -> 19, of which waited for: 9 -> 10; matrix products, arithmetic and copies ran while one was open for 23% -> 6% of each run, Pallas kernels for 0% -> 16%
where the time goes in v2:
time: 143 us; the launch traced here: 142 us
  starting transfers between devices  49.8 us (35%)
  waiting for transfers between devices  44.7 us (31%)
  Pallas kernels  26.1 us (18%)
  other arithmetic  10.2 us (7%)
  local copies, waits for them, and re-layouts  8.51 us (6%)
    ppermute x6, waiting for transfers between devices, from_side(): return lax.ppermute(value, (axis, 'c'), pairs)  18 us
    pallas_call x1, Pallas kernels, head(): pl.pallas_call(head_kernel, in_specs=[pl.BlockSpec(memory_space=pltpu.SME...  13.1 us
    all_to_all x1, starting transfers between devices, per_device(): arrived = lax.all_to_all(send, ALL, split_axis=0, concat_axis=0, tiled=True)  11.7 us
    ppermute x9, starting transfers between devices, shifted(): lax.ppermute(value, axis, [((i + distance) % size, i) for i in range(size)])  11 us
    ppermute x9, waiting for transfers between devices, shifted(): lax.ppermute(value, axis, [((i + distance) % size, i) for i in range(size)])  10.3 us
    ppermute x6, starting transfers between devices, from_side(): return lax.ppermute(value, (axis, 'c'), pairs)  10.2 us
    all_to_all x1, starting transfers between devices, spread(): return lax.all_to_all(copies, axis, split_axis=0, concat_axis=0, tiled=True)  7.59 us
    all_to_all x1, waiting for transfers between devices, per_device(): arrived = lax.all_to_all(send, ALL, split_axis=0, concat_axis=0, tiled=True)  7.21 us
  transfers between devices with their start and end apart: 19, of which 10 were waited for; matrix products, arithmetic and copies ran while one was open for 6% of the time, Pallas kernels for 16%

profile of v2, /device:TPU:1, one launch (start us, length us, event | category | flops | bytes accessed | tf_op | source)
XLA Modules:
  0.0 141.7 jit_solution(10781997679568759218)
XLA Ops:
  0.7 1.4 broadcast_subtract_fusion
  2.1 1.3 broadcast_in_dim.91.gain
  3.4 0.8 pad_maximum_fusion.4
  5.5 4.1 %project.1 = bf16[32,384]{1,0:T(8,128)(2,1)} custom-call(bf16[32,3584]{1,0:T(8,128)(2,1)} %x_ref.1, bf16[1,3584]{1,0:T(2,128)(2,1)} %broadcast_in_dim.91.gain, bf16[1,384]{1,0:T(2,128)(2,1)} %broadcast_in_dim.92.bias, f32[32,64]{1,0:T(8,128)} %get-tuple-element.44.cos, f32[32,64]{1,0:T(8,128)} %get-tuple-element.43.sin, bf16[3584,256]{1,0:T(8,128)(2,1)} %wq_ref.1, ...), custom_call_target="tpu_custom_call" | custom-call | tf_op jit(solution)/shard_map/project/pallas_call | solution.py:190
  9.7 3.3 %collective-permute-start = (bf16[32,384]{1,0:T(8,128)(2,1)}, bf16[32,384]{1,0:T(8,128)(2,1)S(1)}, u32[]{:S(2)}, u32[]{:S(2)}) collective-permute-start(bf16[32,384]{1,0:T(8,128)(2,1)} %project.1), channel_id=1, source_target_pairs={{1,0},{0,1},{3,2},{2,3},{5,4},{4,5},{7,6},{6,7},{9,8},{8,9},{11,10... | collective-permute-start | bytes 73736 | tf_op jit(solution)/shard_map/ppermute | solution.py:16
  13.1 1.0 collective-permute-done
  17.8 1.4 collective-permute-done.1
  20.6 3.7 %all-to-all-start = ((bf16[8,16,896]{2,1,0:T(8,128)(2,1)}), bf16[8,16,896]{2,1,0:T(8,128)(2,1)S(1)}, u32[]{:S(2)}, u32[]{:S(2)}) async-start(bf16[8,16,896]{2,1,0:T(8,128)(2,1)} %bitcast.8), calls=%async_computation | async-start | bytes 458752 | tf_op jit(solution)/shard_map/all_to_all | solution.py:370
  25.7 4.8 %all-to-all-done = bf16[8,16,896]{2,1,0:T(8,128)(2,1)S(1)} async-done(((bf16[8,16,896]{2,1,0:T(8,128)(2,1)}), bf16[8,16,896]{2,1,0:T(8,128)(2,1)S(1)}, u32[]{:S(2)}, u32[]{:S(2)}) %all-to-all-start) | async-done | bytes 229408 | tf_op jit(solution)/shard_map/all_to_all | solution.py:370
  31.9 7.6 %all-to-all-start.1 = ((bf16[8,16,896]{2,1,0:T(8,128)(2,1)}), bf16[8,16,896]{2,1,0:T(8,128)(2,1)S(1)}, u32[]{:S(2)}, u32[]{:S(2)}) async-start(bf16[8,16,896]{2,1,0:T(8,128)(2,1)} %broadcast_in_dim.99), calls=%async_computation.1 | async-start | bytes 458752 | tf_op jit(solution)/shard_map/all_to_all | solution.py:22
  39.5 0.8 convert_reduce_fusion
  41.3 3.3 %pack.1 = bf16[64,128,128]{2,1,0:T(8,128)(2,1)} custom-call(s32[64]{0:T(128)} %select_reduce_fusion.pick, s32[32]{0:T(128)} %get-tuple-element.12.at, bf16[32,1,64,128]{3,2,1,0:T(8,128)(2,1)} %keys.1, bf16[32,1,64,128]{3,2,1,0:T(8,128)(2,1)} %values.1, f32[32,128]{1,0:T(8,128)} %copy-done.7, f32[32,128]{1,0:T(8,128)} %copy-done.8), custom_call_target="tpu_custom_call" | custom-call | tf_op jit(solution)/shard_map/pack/pallas_call | solution.py:224
  44.6 4.4 %all-to-all-done.1 = bf16[8,16,896]{2,1,0:T(8,128)(2,1)S(1)} async-done(((bf16[8,16,896]{2,1,0:T(8,128)(2,1)}), bf16[8,16,896]{2,1,0:T(8,128)(2,1)S(1)}, u32[]{:S(2)}, u32[]{:S(2)}) %all-to-all-start.1) | async-done | bytes 229408 | tf_op jit(solution)/shard_map/all_to_all | solution.py:22
  49.0 5.7 %all-to-all-start.2 = ((bf16[64,128,128]{2,1,0:T(8,128)(2,1)}), bf16[64,128,128]{2,1,0:T(8,128)(2,1)}, u32[]{:S(2)}, u32[]{:S(2)}) async-start(bf16[64,128,128]{2,1,0:T(8,128)(2,1)} %pack.1), calls=%async_computation.2 | async-start | bytes 4194304 | tf_op jit(solution)/shard_map/all_to_all | solution.py:408
  54.7 1.0 collective-permute-start.8
  55.7 1.2 collective-permute-start.9
  57.1 2.5 %collective-permute-start.2 = (bf16[64,896]{1,0:T(8,128)(2,1)S(1)}, bf16[64,896]{1,0:T(8,128)(2,1)S(1)}, u32[]{:S(2)}, u32[]{:S(2)}) collective-permute-start(bf16[64,896]{1,0:T(8,128)(2,1)S(1)} %get-tuple-element.24), channel_id=1, source_target_pairs={{64,0},{128,64},{192,128},{0,192},{65,1},{129,65},{193,129},{1,193... | collective-permute-start | bytes 344072 | tf_op jit(solution)/shard_map/ppermute | solution.py:16
  59.6 1.9 %collective-permute-start.3 = (bf16[64,896]{1,0:T(8,128)(2,1)S(1)}, bf16[64,896]{1,0:T(8,128)(2,1)S(1)}, u32[]{:S(2)}, u32[]{:S(2)}) collective-permute-start(bf16[64,896]{1,0:T(8,128)(2,1)S(1)} %get-tuple-element.24), channel_id=1, source_target_pairs={{128,0},{192,64},{0,128},{64,192},{129,1},{193,65},{1,129},{65,193... | collective-permute-start | bytes 344072 | tf_op jit(solution)/shard_map/ppermute | solution.py:16
  62.5 1.2 collective-permute-start.11
  63.8 2.3 %collective-permute-done.3 = bf16[64,896]{1,0:T(8,128)(2,1)S(1)} collective-permute-done((bf16[64,896]{1,0:T(8,128)(2,1)S(1)}, bf16[64,896]{1,0:T(8,128)(2,1)S(1)}, u32[]{:S(2)}, u32[]{:S(2)}) %collective-permute-start.3) | collective-permute-done | bytes 114720 | tf_op jit(solution)/shard_map/ppermute | solution.py:16
  66.1 5.2 %collective-permute-done.4 = bf16[64,896]{1,0:T(8,128)(2,1)S(1)} collective-permute-done((bf16[64,896]{1,0:T(8,128)(2,1)S(1)}, bf16[64,896]{1,0:T(8,128)(2,1)S(1)}, u32[]{:S(2)}, u32[]{:S(2)}) %collective-permute-start.4) | collective-permute-done | bytes 114720 | tf_op jit(solution)/shard_map/ppermute | solution.py:16
  71.4 3.4 %collective-permute-start.5 = (bf16[4,64,896]{2,1,0:T(8,128)(2,1)S(1)}, bf16[4,64,896]{2,1,0:T(8,128)(2,1)}, u32[]{:S(2)}, u32[]{:S(2)}) collective-permute-start(bf16[4,64,896]{2,1,0:T(8,128)(2,1)S(1)} %pad_maximum_fusion.refs_0_), channel_id=1, source_target_pairs={{2,0},{7,1},{4,2},{1,3},{6,4},{3,5},{0,6},{5,7},{10,8},{15,9},{12,... | collective-permute-start | bytes 1376264 | tf_op jit(solution)/shard_map/ppermute | solution.py:41
  75.1 1.6 %collective-permute-start.7 = (bf16[4,64,896]{2,1,0:T(8,128)(2,1)S(1)}, bf16[4,64,896]{2,1,0:T(8,128)(2,1)}, u32[]{:S(2)}, u32[]{:S(2)}) collective-permute-start(bf16[4,64,896]{2,1,0:T(8,128)(2,1)S(1)} %pad_maximum_fusion.refs_0_), channel_id=1, source_target_pairs={{6,0},{3,1},{0,2},{5,3},{2,4},{7,5},{4,6},{1,7},{14,8},{11,9},{8,1... | collective-permute-start | bytes 1376264 | tf_op jit(solution)/shard_map/ppermute | solution.py:41
  76.8 5.7 %collective-permute-done.11.refs_5_ = bf16[4,64,896]{2,1,0:T(8,128)(2,1)S(1)} collective-permute-done((bf16[4,64,896]{2,1,0:T(8,128)(2,1)S(1)}, bf16[4,64,896]{2,1,0:T(8,128)(2,1)S(1)}, u32[]{:S(2)}, u32[]{:S(2)}) %collective-permute-start.11) | collective-permute-done | bytes 458784 | tf_op jit(solution)/shard_map/ppermute | solution.py:41
  82.5 3.6 %collective-permute-start.12 = (bf16[4,64,896]{2,1,0:T(8,128)(2,1)S(1)}, bf16[4,64,896]{2,1,0:T(8,128)(2,1)}, u32[]{:S(2)}, u32[]{:S(2)}) collective-permute-start(bf16[4,64,896]{2,1,0:T(8,128)(2,1)S(1)} %collective-permute-done.11.refs_5_), channel_id=1, source_target_pairs={{64,0},{193,1},{128,64},{1,65},{192,128},{65,129},{0,192},{129,193... | collective-permute-start | bytes 1376264 | tf_op jit(solution)/shard_map/ppermute | solution.py:41
  87.3 0.8 reshape.293.refs_10_
  89.3 12.3 %collective-permute-done.12.refs_6_ = bf16[4,64,896]{2,1,0:T(8,128)(2,1)} collective-permute-done((bf16[4,64,896]{2,1,0:T(8,128)(2,1)S(1)}, bf16[4,64,896]{2,1,0:T(8,128)(2,1)}, u32[]{:S(2)}, u32[]{:S(2)}) %collective-permute-start.12) | collective-permute-done | bytes 458784 | tf_op jit(solution)/shard_map/ppermute | solution.py:41
  101.6 13.1 %head.1.value = f32[256,128]{1,0:T(8,128)} custom-call(s32[2,4]{1,0:T(2,128)} %pad_add_fusion.4.y_ref, bf16[4,64,896]{2,1,0:T(8,128)(2,1)} %copy-done.4, bf16[4,64,896]{2,1,0:T(8,128)(2,1)} %collective-permute-done.5.refs_1_, bf16[4,64,896]{2,1,0:T(8,128)(2,1)} %collective-permute-done.6.refs_2_, bf16[4,64,896]{2,1,0:T(8,128)(2,1)} %collective-permute-done.7.refs_3_, ...), custom_call_target="tpu_custom_call" | custom-call | tf_op jit(solution)/shard_map/head/pallas_call | solution.py:115
  114.7 11.7 %all-to-all-start.3 = ((f32[256,1,128]{2,1,0:T(1,128)}), f32[256,1,128]{2,1,0:T(1,128)S(1)}, u32[]{:S(2)}, u32[]{:S(2)}) async-start(f32[256,1,128]{2,1,0:T(1,128)} %bitcast.59), calls=%async_computation.3 | async-start | bytes 262144 | tf_op jit(solution)/shard_map/all_to_all | solution.py:411
  126.4 5.6 %settle.1 = (bf16[64,1,64,128]{3,2,1,0:T(8,128)(2,1)}, bf16[64,1,64,128]{3,2,1,0:T(8,128)(2,1)}) custom-call(bf16[64,128,128]{2,1,0:T(8,128)(2,1)} %all-to-all-done.2.other.got), custom_call_target="tpu_custom_call" | custom-call | tf_op jit(solution)/shard_map/settle/pallas_call | solution.py:244
  132.0 7.2 %all-to-all-done.3.value = f32[256,1,128]{2,1,0:T(1,128)S(1)} async-done(((f32[256,1,128]{2,1,0:T(1,128)}), f32[256,1,128]{2,1,0:T(1,128)S(1)}, u32[]{:S(2)}, u32[]{:S(2)}) %all-to-all-start.3) | async-done | bytes 131104 | tf_op jit(solution)/shard_map/all_to_all | solution.py:411
  139.9 1.2 fusion.3
  (119 shorter events, 15.6 us)
Async XLA Ops:
  0.6 18.7 %copy-start = (bf16[256,3584]{1,0:T(8,128)(2,1)S(1)}, bf16[256,3584]{1,0:T(8,128)(2,1)}, u32[]{:S(2)}) copy-start(bf16[256,3584]{1,0:T(8,128)(2,1)} %param.28) | copy-start | bytes 5505028
  3.4 12.0 %copy-start.2 = (bf16[32,1,64,128]{3,2,1,0:T(8,128)(2,1)S(1)}, bf16[32,1,64,128]{3,2,1,0:T(8,128)(2,1)}, u32[]{:S(2)}) copy-start(bf16[32,1,64,128]{3,2,1,0:T(8,128)(2,1)} %keys.1) | copy-start | bytes 1572868
  5.5 10.7 %copy-start.5 = (bf16[32,1,64,128]{3,2,1,0:T(8,128)(2,1)S(1)}, bf16[32,1,64,128]{3,2,1,0:T(8,128)(2,1)}, u32[]{:S(2)}) copy-start(bf16[32,1,64,128]{3,2,1,0:T(8,128)(2,1)} %values.1) | copy-start | bytes 1572868
  9.7 4.4 %collective-permute-start = (bf16[32,384]{1,0:T(8,128)(2,1)}, bf16[32,384]{1,0:T(8,128)(2,1)S(1)}, u32[]{:S(2)}, u32[]{:S(2)}) collective-permute-start(bf16[32,384]{1,0:T(8,128)(2,1)} %project.1), channel_id=1, source_target_pairs={{1,0},{0,1},{3,2},{2,3},{5,4},{4,5},{7,6},{6,7},{9,8},{8,9},{11,10... | collective-permute-start | bytes 73736 | tf_op jit(solution)/shard_map/ppermute | solution.py:16
  15.2 2.0 %copy-start.7 = (f32[32,128]{1,0:T(8,128)}, f32[32,128]{1,0:T(8,128)S(1)}, u32[]{:S(2)}) copy-start(f32[32,128]{1,0:T(8,128)S(1)} %maximum_convert_fusion.1.key_new) | copy-start | bytes 49156
  16.2 1.1 copy-start.8
  17.3 1.8 %collective-permute-start.1 = (f32[32,2,384]{0,1,2:T(2,128)S(1)}, f32[32,2,384]{0,1,2:T(2,128)S(1)}, u32[]{:S(2)}, u32[]{:S(2)}) collective-permute-start(f32[32,2,384]{0,1,2:T(2,128)S(1)} %bitcast.64), channel_id=1, source_target_pairs={{1,0},{0,1},{3,2},{2,3},{5,4},{4,5},{7,6},{6,7},{9,8},{8,9},{11,10... | collective-permute-start | bytes 294920 | tf_op jit(solution)/shard_map/ppermute | solution.py:16
  19.2 5.7 %copy-start.10 = (s32[1024,1]{0,1:T(1,128)S(1)}, s32[1024,1]{0,1:T(1,128)}, u32[]{:S(2)}) copy-start(s32[1024,1]{0,1:T(1,128)} %param.21) | copy-start | bytes 12292
  20.6 9.9 %all-to-all-start = ((bf16[8,16,896]{2,1,0:T(8,128)(2,1)}), bf16[8,16,896]{2,1,0:T(8,128)(2,1)S(1)}, u32[]{:S(2)}, u32[]{:S(2)}) async-start(bf16[8,16,896]{2,1,0:T(8,128)(2,1)} %bitcast.8), calls=%async_computation | async-start | bytes 458752 | tf_op jit(solution)/shard_map/all_to_all | solution.py:370
  24.2 77.4 %collective-permute-start.14 = (bf16[594,3584]{1,0:T(8,128)(2,1)}, bf16[594,3584]{1,0:T(8,128)(2,1)}, u32[]{:S(2)}, u32[]{:S(2)}) collective-permute-start(bf16[594,3584]{1,0:T(8,128)(2,1)} %refs_11_.1), channel_id=1, source_target_pairs={{1,0},{0,1},{3,2},{2,3},{5,4},{4,5},{7,6},{6,7},{9,8},{8,9},{11,10... | collective-permute-start | bytes 12773384 | tf_op jit(solution)/shard_map/ppermute | solution.py:16
  31.9 17.0 %all-to-all-start.1 = ((bf16[8,16,896]{2,1,0:T(8,128)(2,1)}), bf16[8,16,896]{2,1,0:T(8,128)(2,1)S(1)}, u32[]{:S(2)}, u32[]{:S(2)}) async-start(bf16[8,16,896]{2,1,0:T(8,128)(2,1)} %broadcast_in_dim.99), calls=%async_computation.1 | async-start | bytes 458752 | tf_op jit(solution)/shard_map/all_to_all | solution.py:22
  49.0 65.7 %all-to-all-start.2 = ((bf16[64,128,128]{2,1,0:T(8,128)(2,1)}), bf16[64,128,128]{2,1,0:T(8,128)(2,1)}, u32[]{:S(2)}, u32[]{:S(2)}) async-start(bf16[64,128,128]{2,1,0:T(8,128)(2,1)} %pack.1), calls=%async_computation.2 | async-start | bytes 4194304 | tf_op jit(solution)/shard_map/all_to_all | solution.py:408
  54.7 33.4 %copy-start.9 = (bf16[3584]{0:T(1024)(128)(2,1)S(1)}, bf16[3584]{0:T(1024)(128)(2,1)}, u32[]{:S(2)}) copy-start(bf16[3584]{0:T(1024)(128)(2,1)} %param.30) | copy-start | bytes 21508
  54.7 4.9 %collective-permute-start.8 = (bf16[64,896]{1,0:T(8,128)(2,1)S(1)}, bf16[64,896]{1,0:T(8,128)(2,1)S(1)}, u32[]{:S(2)}, u32[]{:S(2)}) collective-permute-start(bf16[64,896]{1,0:T(8,128)(2,1)S(1)} %get-tuple-element.25), channel_id=1, source_target_pairs={{2,0},{4,2},{6,4},{0,6},{3,1},{5,3},{7,5},{1,7},{10,8},{12,10},{14... | collective-permute-start | bytes 344072 | tf_op jit(solution)/shard_map/ppermute | solution.py:16
  55.7 5.8 %collective-permute-start.9 = (bf16[64,896]{1,0:T(8,128)(2,1)S(1)}, bf16[64,896]{1,0:T(8,128)(2,1)S(1)}, u32[]{:S(2)}, u32[]{:S(2)}) collective-permute-start(bf16[64,896]{1,0:T(8,128)(2,1)S(1)} %get-tuple-element.25), channel_id=1, source_target_pairs={{4,0},{6,2},{0,4},{2,6},{5,1},{7,3},{1,5},{3,7},{12,8},{14,10},{8,... | collective-permute-start | bytes 344072 | tf_op jit(solution)/shard_map/ppermute | solution.py:16
  56.9 5.6 %collective-permute-start.10 = (bf16[64,896]{1,0:T(8,128)(2,1)S(1)}, bf16[64,896]{1,0:T(8,128)(2,1)S(1)}, u32[]{:S(2)}, u32[]{:S(2)}) collective-permute-start(bf16[64,896]{1,0:T(8,128)(2,1)S(1)} %get-tuple-element.25), channel_id=1, source_target_pairs={{6,0},{0,2},{2,4},{4,6},{7,1},{1,3},{3,5},{5,7},{14,8},{8,10},{10,... | collective-permute-start | bytes 344072 | tf_op jit(solution)/shard_map/ppermute | solution.py:16
  57.1 6.6 %collective-permute-start.2 = (bf16[64,896]{1,0:T(8,128)(2,1)S(1)}, bf16[64,896]{1,0:T(8,128)(2,1)S(1)}, u32[]{:S(2)}, u32[]{:S(2)}) collective-permute-start(bf16[64,896]{1,0:T(8,128)(2,1)S(1)} %get-tuple-element.24), channel_id=1, source_target_pairs={{64,0},{128,64},{192,128},{0,192},{65,1},{129,65},{193,129},{1,193... | collective-permute-start | bytes 344072 | tf_op jit(solution)/shard_map/ppermute | solution.py:16
  59.6 6.5 %collective-permute-start.3 = (bf16[64,896]{1,0:T(8,128)(2,1)S(1)}, bf16[64,896]{1,0:T(8,128)(2,1)S(1)}, u32[]{:S(2)}, u32[]{:S(2)}) collective-permute-start(bf16[64,896]{1,0:T(8,128)(2,1)S(1)} %get-tuple-element.24), channel_id=1, source_target_pairs={{128,0},{192,64},{0,128},{64,192},{129,1},{193,65},{1,129},{65,193... | collective-permute-start | bytes 344072 | tf_op jit(solution)/shard_map/ppermute | solution.py:16
  61.5 9.8 %collective-permute-start.4 = (bf16[64,896]{1,0:T(8,128)(2,1)S(1)}, bf16[64,896]{1,0:T(8,128)(2,1)S(1)}, u32[]{:S(2)}, u32[]{:S(2)}) collective-permute-start(bf16[64,896]{1,0:T(8,128)(2,1)S(1)} %get-tuple-element.24), channel_id=1, source_target_pairs={{192,0},{0,64},{64,128},{128,192},{193,1},{1,65},{65,129},{129,193... | collective-permute-start | bytes 344072 | tf_op jit(solution)/shard_map/ppermute | solution.py:16
  62.5 39.0 %copy-start.3 = (bf16[4,64,896]{2,1,0:T(8,128)(2,1)}, bf16[4,64,896]{2,1,0:T(8,128)(2,1)S(1)}, u32[]{:S(2)}) copy-start(bf16[4,64,896]{2,1,0:T(8,128)(2,1)S(1)} %pad_maximum_fusion.1.refs_4_) | copy-start | bytes 1376260
  62.5 19.9 %collective-permute-start.11 = (bf16[4,64,896]{2,1,0:T(8,128)(2,1)S(1)}, bf16[4,64,896]{2,1,0:T(8,128)(2,1)S(1)}, u32[]{:S(2)}, u32[]{:S(2)}) collective-permute-start(bf16[4,64,896]{2,1,0:T(8,128)(2,1)S(1)} %pad_maximum_fusion.1.refs_4_), channel_id=1, source_target_pairs={{64,0},{193,1},{128,64},{1,65},{192,128},{65,129},{0,192},{129,193... | collective-permute-start | bytes 1376264 | tf_op jit(solution)/shard_map/ppermute | solution.py:41
  71.4 30.2 %copy-start.4 = (bf16[4,64,896]{2,1,0:T(8,128)(2,1)}, bf16[4,64,896]{2,1,0:T(8,128)(2,1)S(1)}, u32[]{:S(2)}) copy-start(bf16[4,64,896]{2,1,0:T(8,128)(2,1)S(1)} %pad_maximum_fusion.refs_0_) | copy-start | bytes 1376260
  71.4 14.7 %collective-permute-start.5 = (bf16[4,64,896]{2,1,0:T(8,128)(2,1)S(1)}, bf16[4,64,896]{2,1,0:T(8,128)(2,1)}, u32[]{:S(2)}, u32[]{:S(2)}) collective-permute-start(bf16[4,64,896]{2,1,0:T(8,128)(2,1)S(1)} %pad_maximum_fusion.refs_0_), channel_id=1, source_target_pairs={{2,0},{7,1},{4,2},{1,3},{6,4},{3,5},{0,6},{5,7},{10,8},{15,9},{12,... | collective-permute-start | bytes 1376264 | tf_op jit(solution)/shard_map/ppermute | solution.py:41
  75.1 14.2 %collective-permute-start.13 = (bf16[4,64,896]{2,1,0:T(8,128)(2,1)S(1)}, bf16[4,64,896]{2,1,0:T(8,128)(2,1)}, u32[]{:S(2)}, u32[]{:S(2)}) collective-permute-start(bf16[4,64,896]{2,1,0:T(8,128)(2,1)S(1)} %pad_maximum_fusion.1.refs_4_), channel_id=1, source_target_pairs={{192,0},{65,1},{0,64},{129,65},{64,128},{193,129},{128,192},{1,193... | collective-permute-start | bytes 1376264 | tf_op jit(solution)/shard_map/ppermute | solution.py:41
  75.1 14.1 %collective-permute-start.7 = (bf16[4,64,896]{2,1,0:T(8,128)(2,1)S(1)}, bf16[4,64,896]{2,1,0:T(8,128)(2,1)}, u32[]{:S(2)}, u32[]{:S(2)}) collective-permute-start(bf16[4,64,896]{2,1,0:T(8,128)(2,1)S(1)} %pad_maximum_fusion.refs_0_), channel_id=1, source_target_pairs={{6,0},{3,1},{0,2},{5,3},{2,4},{7,5},{4,6},{1,7},{14,8},{11,9},{8,1... | collective-permute-start | bytes 1376264 | tf_op jit(solution)/shard_map/ppermute | solution.py:41
  82.5 19.1 %copy-start.6 = (bf16[4,64,896]{2,1,0:T(8,128)(2,1)}, bf16[4,64,896]{2,1,0:T(8,128)(2,1)S(1)}, u32[]{:S(2)}) copy-start(bf16[4,64,896]{2,1,0:T(8,128)(2,1)S(1)} %collective-permute-done.11.refs_5_) | copy-start | bytes 1376260
  82.5 19.1 %collective-permute-start.12 = (bf16[4,64,896]{2,1,0:T(8,128)(2,1)S(1)}, bf16[4,64,896]{2,1,0:T(8,128)(2,1)}, u32[]{:S(2)}, u32[]{:S(2)}) collective-permute-start(bf16[4,64,896]{2,1,0:T(8,128)(2,1)S(1)} %collective-permute-done.11.refs_5_), channel_id=1, source_target_pairs={{64,0},{193,1},{128,64},{1,65},{192,128},{65,129},{0,192},{129,193... | collective-permute-start | bytes 1376264 | tf_op jit(solution)/shard_map/ppermute | solution.py:41
  86.1 15.5 %collective-permute-start.6 = (bf16[4,64,896]{2,1,0:T(8,128)(2,1)}, bf16[4,64,896]{2,1,0:T(8,128)(2,1)}, u32[]{:S(2)}, u32[]{:S(2)}) collective-permute-start(bf16[4,64,896]{2,1,0:T(8,128)(2,1)} %collective-permute-done.5.refs_1_), channel_id=1, source_target_pairs={{2,0},{7,1},{4,2},{1,3},{6,4},{3,5},{0,6},{5,7},{10,8},{15,9},{12,... | collective-permute-start | bytes 1376264 | tf_op jit(solution)/shard_map/ppermute | solution.py:41
  114.7 24.5 %all-to-all-start.3 = ((f32[256,1,128]{2,1,0:T(1,128)}), f32[256,1,128]{2,1,0:T(1,128)S(1)}, u32[]{:S(2)}, u32[]{:S(2)}) async-start(f32[256,1,128]{2,1,0:T(1,128)} %bitcast.59), calls=%async_computation.3 | async-start | bytes 262144 | tf_op jit(solution)/shard_map/all_to_all | solution.py:411
  139.2 0.7 copy-start.1

commit v3 on v2

--- a/solution.py
+++ b/solution.py
@@ -9,6 +9,7 @@
 TP = ("y", "c")
 ALL = ("x", "z", "y", "c")
 HBM = pltpu.MemorySpace.HBM
+PER = 8
 
 
 def shifted(value, axis, distance):
@@ -69,23 +70,25 @@
         copy.start()
     n, quarter, cols = landed[0].shape
     sums = [0.0] * (2 * n)
-    for copy in copies:
-        copy.wait()
-    for load in loads:
-        load.start()
+    def put(i, piece, chunk):
+        start = pl.multiple_of(chunk * cols, 128)
+        scale = gain[:, pl.ds(start, cols)].astype(f32)
+        wide = piece.astype(f32)
+        sums[i] = sums[i] + jnp.sum(wide * wide, axis=1, keepdims=True)
+        x[pl.ds(i * quarter, quarter), pl.ds(start, cols)] = (wide * scale).astype(bf16)
+
     for d in range(n):
-        start_a = pl.multiple_of(y_ref[1, d] * cols, 128)
-        start_b = pl.multiple_of(y_ref[0, d] * cols, 128)
-        scale_a = gain[:, pl.ds(start_a, cols)].astype(f32)
-        scale_b = gain[:, pl.ds(start_b, cols)].astype(f32)
-        for i in range(2 * n):
-            if i < n:
-                piece, start, scale = landed[d][i], start_a, scale_a
-            else:
-                piece, start, scale = landed[i][d], start_b, scale_b
-            wide = piece.astype(f32)
-            sums[i] = sums[i] + jnp.sum(wide * wide, axis=1, keepdims=True)
-            x[pl.ds(i * quarter, quarter), pl.ds(start, cols)] = (wide * scale).astype(bf16)
+        copies[d].wait()
+        for i in range(n):
+            put(i, landed[d][i], y_ref[1, d])
+    loads[0].start()
+    for i in range(n):
+        copies[n + i].wait()
+        for d in range(n):
+            put(n + i, landed[n + i][d], y_ref[0, d])
+        if i == 0:
+            for load in loads[1:]:
+                load.start()
     dims = (((1,), (1,)), ((), ()))
     top = None
     for load, (i, low, high) in zip(loads, tiles):
@@ -95,15 +98,25 @@
         top = peak if top is None else jnp.maximum(top, peak)
 
     ms = jnp.concatenate(sums, axis=0) / width
+    top = jnp.transpose(jnp.broadcast_to(top, (8, top.shape[1])))[:, :1]
+    at = lane[...]
+    lanes = lax.broadcasted_iota(jnp.int32, (ms.shape[0], out.shape[1]), 1) - at
+    spots = (lanes == 6 * PER).astype(f32)
+    for i, value in enumerate((top, ms)):
+        for j in range(3):
+            term = value.astype(bf16).astype(f32)
+            spots = spots + jnp.where(lanes == (3 * i + j) * PER, term, 0.0)
+            value = value - term
     here = lax.broadcasted_iota(jnp.int32, (out.shape[0], row.shape[1]), 0) == row[...]
-    lanes = lax.broadcasted_iota(jnp.int32, (row.shape[1], out.shape[1]), 1)
-    at = lane[...]
-    place = (lanes == at).astype(f32)
-    rest = jnp.where(lanes == at + 8, ms, 0.0) + (lanes == at + 16).astype(f32)
-    exact = lax.Precision.HIGHEST
-    out[...] = jnp.dot(
-        jnp.where(here, top, 0.0), place, precision=exact, preferred_element_type=f32
-    ) + jnp.dot(here.astype(f32), rest, precision=exact, preferred_element_type=f32)
+    moved = jnp.dot(here.astype(bf16), spots.astype(bf16), preferred_element_type=f32)
+
+    def turned(terms):
+        return pltpu.roll(moved, moved.shape[1] - terms * PER, 1)
+
+    values = moved + turned(1) + turned(2)
+    is_top = lax.broadcasted_iota(jnp.int32, out.shape, 1) < PER
+    absent = is_top & (turned(6) == 0.0)
+    out[...] = jnp.where(absent, -jnp.inf, values)
 
 
 def head(y_pos, chunks_a, chunks_b, gain, row, lane, own, other, targets):
@@ -160,7 +173,11 @@
         load.start()
     x = x_ref[...].astype(f32)
     mean = jnp.mean(x * x, axis=1, keepdims=True)
-    normed = (x * lax.rsqrt(mean + 1e-06) * gain[...].astype(f32)).astype(bf16)
+    scale = gain[...].astype(f32)
+    scale = jnp.concatenate([scale[i : i + 1] for i in range(scale.shape[0])], axis=1)
+    normed = (x * lax.rsqrt(mean + 1e-06) * scale).astype(bf16)
+    terms = bias[...].astype(f32)
+    terms = jnp.concatenate([terms[i : i + 1] for i in range(terms.shape[0])], axis=1)
     for load in loads:
         load.wait()
     query = jnp.dot(normed, wq[...], preferred_element_type=f32)
@@ -172,14 +189,14 @@
     c, s = cos[...], sin[...]
     half = c.shape[1]
     at = query.shape[1]
-    query = query + bias[:, :at].astype(f32)
+    query = query + terms[:, :at]
     for low in range(0, at, 2 * half):
         first = query[:, low : low + half]
         second = query[:, low + half : low + 2 * half]
         out[:, low : low + 2 * half] = jnp.concatenate(
             [first * c - second * s, second * c + first * s], axis=1
         ).astype(bf16)
-    out[:, at:] = (jnp.concatenate(rest, axis=1) + bias[:, at:].astype(f32)).astype(bf16)
+    out[:, at:] = (jnp.concatenate(rest, axis=1) + terms[:, at:]).astype(bf16)
 
 
 def project(x, gain, wq, bq, wk, bk, wv, bv, cos, sin):
@@ -196,7 +213,7 @@
         + [pltpu.SemaphoreType.DMA((3,))],
         compiler_params=pltpu.CompilerParams(vmem_limit_bytes=60 * 1024 * 1024),
         name="project",
-    )(x, gain[None], jnp.concatenate([bq, bk, bv])[None], cos, sin, *weights)
+    )(x, gain.reshape(-1, 128), jnp.concatenate([bq, bk, bv]).reshape(-1, 128), cos, sin, *weights)
 
 
 def pack_kernel(pick, at, keys, values, key_new, value_new, out):
@@ -374,21 +391,27 @@
     n_x = lax.axis_size("x")
     part = rows // 2
     by_z = spread(state, "z")
+    part_b = by_z[:, part:].reshape(n_z * part, cols)
     part_a = by_z[:, :part].reshape(n_z * part, cols)
-    part_b = by_z[:, part:].reshape(n_z * part, cols)
-    from_x = [part_a] + [shifted(part_a, "x", d) for d in range(1, n_x)]
     from_y = [part_b] + [shifted(part_b, "y", d) for d in range(1, n_y)]
+    late_a = after(part_a, from_y[1])
+    from_x = [part_a] + [shifted(late_a, "x", d) for d in range(1, n_x)]
     by_z = after(by_z, send_kv)
+    block_b = jnp.stack(from_y)
     block_a = jnp.stack(from_x)
-    block_b = jnp.stack(from_y)
+    chunks_b = ring(block_b, "x")
     chunks_a = ring(block_a, "y")
-    chunks_b = ring(block_b, "x")
     own_rows = lax.dynamic_slice(bucket, (0, c_pos * rows), (n_rep, rows))
     source = jnp.arange(n_rep, dtype=jnp.int32)[:, None]
     per_tp = n_rep // n_tp
     row = own_rows // cap * n_tp + source // per_tp
     lane = source % per_tp * cap + own_rows % cap
 
+    tp_pos = y_pos * 2 + c_pos
+    feeding = lax.dynamic_slice(bucket, (tp_pos * per_tp, 0), (per_tp, slots))
+    own_buckets = rep_pos * cap + jnp.arange(cap, dtype=jnp.int32)
+    taken = jnp.any(feeding[:, None, :] == own_buckets[None, :, None], axis=2).reshape(-1)
+
     def in_chunk_order(table):
         table = table.reshape(n_x, n_z, 2, part).transpose(2, 0, 1, 3)
         table = jnp.roll(table, -lax.axis_index("x"), axis=1)
@@ -409,12 +432,9 @@
     keys_out, values_out = settle(got)
     send = after(send, got)[:, None]
     arrived = lax.all_to_all(send, ALL, split_axis=0, concat_axis=0, tiled=True)
-    arrived = after(arrived, keys_out)[:, 0]
-    slots_here = per_tp * cap
-    present = arrived[:, 2 * slots_here : 3 * slots_here] > 0.0
-    best = jnp.max(jnp.where(present, arrived[:, :slots_here], -jnp.inf), axis=0)
-    ms = jnp.max(arrived[:, slots_here : 2 * slots_here], axis=0)
-    taken = jnp.any(present, axis=0)
+    arrived = jnp.max(after(arrived, keys_out), axis=(0, 1))
+    best = arrived[:PER]
+    ms = arrived[3 * PER : 4 * PER]
     final_norm = jnp.where(taken, jnp.sqrt(ms), 0.0)
     top_logit = jnp.where(taken, best * lax.rsqrt(ms + eps), 0.0)
     return (final_norm, top_logit, keys_out, values_out)

time: 143 us -> 141 us (0.986)
  Pallas kernels: 26.1 us -> 24.1 us
  starting transfers between devices: 49.8 us -> 47.8 us
  other arithmetic: 10.2 us -> 11.9 us
    ppermute x6, waiting for transfers between devices: 18 us -> 21.4 us  [from_side(): return lax.ppermute(value, (axis, 'c'), pairs)]
    ppermute x6, starting transfers between devices: 10.2 us -> 7.22 us  [from_side(): return lax.ppermute(value, (axis, 'c'), pairs)]
    pallas_call x1, Pallas kernels: 13.1 us -> 11 us  [head(): pl.pallas_call(head_kernel, in_specs=[pl.BlockSpec(memory_space=pltpu.SME...]
    ppermute x9, waiting for transfers between devices: 10.3 us -> 8.44 us  [shifted(): lax.ppermute(value, axis, [((i + distance) % size, i) for i in range(size)])]
    broadcast_in_dim x2 -> x0, local copies, waits for them, and re-layouts: 1.87 us -> none  [the longest x1 1.3 us: project(): gain[None]]
  transfers between devices with their start and end apart: 19 -> 19, of which waited for: 10 -> 10; matrix products, arithmetic and copies ran while one was open for 6% -> 7% of each run, Pallas kernels for 16% -> 14%
where the time goes in v3:
time: 141 us; the launch traced here: 140 us
  starting transfers between devices  47.8 us (34%)
  waiting for transfers between devices  45.6 us (32%)
  Pallas kernels  24.1 us (17%)
  other arithmetic  11.9 us (8%)
  local copies, waits for them, and re-layouts  8.28 us (6%)
    ppermute x6, waiting for transfers between devices, from_side(): return lax.ppermute(value, (axis, 'c'), pairs)  21.4 us
    all_to_all x1, starting transfers between devices, per_device(): arrived = lax.all_to_all(send, ALL, split_axis=0, concat_axis=0, tiled=True)  12.2 us
    ppermute x9, starting transfers between devices, shifted(): lax.ppermute(value, axis, [((i + distance) % size, i) for i in range(size)])  11.4 us
    pallas_call x1, Pallas kernels, head(): pl.pallas_call(head_kernel, in_specs=[pl.BlockSpec(memory_space=pltpu.SME...  11 us
    ppermute x9, waiting for transfers between devices, shifted(): lax.ppermute(value, axis, [((i + distance) % size, i) for i in range(size)])  8.44 us
    all_to_all x1, starting transfers between devices, spread(): return lax.all_to_all(copies, axis, split_axis=0, concat_axis=0, tiled=True)  7.59 us
    ppermute x6, starting transfers between devices, from_side(): return lax.ppermute(value, (axis, 'c'), pairs)  7.22 us
    all_to_all x1, waiting for transfers between devices, per_device(): arrived = lax.all_to_all(send, ALL, split_axis=0, concat_axis=0, tiled=True)  6.65 us
  transfers between devices with their start and end apart: 19, of which 10 were waited for; matrix products, arithmetic and copies ran while one was open for 7% of the time, Pallas kernels for 14%

profile of v3, /device:TPU:1, one launch (start us, length us, event | category | flops | bytes accessed | tf_op | source)
XLA Modules:
  0.0 140.0 jit_solution(3250263154498432398)
XLA Ops:
  0.7 1.4 %broadcast_subtract_fusion = (s32[32]{0:T(128)}, s32[32]{0:T(128)S(1)}) fusion(s32[]{:T(128)S(6)} %mul.155, s32[1024]{0:T(1024)} %param.20, s32[]{:T(128)S(6)} %select_n.190), kind=kLoop, calls=%fused_computation.108 | loop fusion | flops 32 | bytes 392 | tf_op jit(solution)/shard_map/sub | solution.py:382
  2.9 1.3 maximum_bitcast_fusion.bias
  4.2 4.1 %project.1 = bf16[32,384]{1,0:T(8,128)(2,1)} custom-call(bf16[32,3584]{1,0:T(8,128)(2,1)} %x_ref.1, bf16[28,128]{1,0:T(8,128)(2,1)} %bitcast.75, bf16[3,128]{1,0:T(4,128)(2,1)} %maximum_bitcast_fusion.bias, f32[32,64]{1,0:T(8,128)} %get-tuple-element.41.cos, f32[32,64]{1,0:T(8,128)} %get-tuple-element.40.sin, bf16[3584,256]{1,0:T(8,128)(2,1)} %wq_ref.1, ...), custom_call_target="tpu_custom_call" | custom-call | tf_op jit(solution)/shard_map/project/pallas_call | solution.py:207
  8.3 3.3 %collective-permute-start = (bf16[32,384]{1,0:T(8,128)(2,1)}, bf16[32,384]{1,0:T(8,128)(2,1)S(1)}, u32[]{:S(2)}, u32[]{:S(2)}) collective-permute-start(bf16[32,384]{1,0:T(8,128)(2,1)} %project.1), channel_id=1, source_target_pairs={{1,0},{0,1},{3,2},{2,3},{5,4},{4,5},{7,6},{6,7},{9,8},{8,9},{11,10... | collective-permute-start | bytes 73736 | tf_op jit(solution)/shard_map/ppermute | solution.py:17
  11.8 1.0 collective-permute-done
  16.4 1.4 collective-permute-done.1
  19.2 3.6 %all-to-all-start = ((bf16[8,16,896]{2,1,0:T(8,128)(2,1)}), bf16[8,16,896]{2,1,0:T(8,128)(2,1)S(1)}, u32[]{:S(2)}, u32[]{:S(2)}) async-start(bf16[8,16,896]{2,1,0:T(8,128)(2,1)} %bitcast.10), calls=%async_computation | async-start | bytes 458752 | tf_op jit(solution)/shard_map/all_to_all | solution.py:387
  24.4 4.8 %all-to-all-done = bf16[8,16,896]{2,1,0:T(8,128)(2,1)S(1)} async-done(((bf16[8,16,896]{2,1,0:T(8,128)(2,1)}), bf16[8,16,896]{2,1,0:T(8,128)(2,1)S(1)}, u32[]{:S(2)}, u32[]{:S(2)}) %all-to-all-start) | async-done | bytes 229408 | tf_op jit(solution)/shard_map/all_to_all | solution.py:387
  30.6 7.6 %all-to-all-start.1 = ((bf16[8,16,896]{2,1,0:T(8,128)(2,1)}), bf16[8,16,896]{2,1,0:T(8,128)(2,1)S(1)}, u32[]{:S(2)}, u32[]{:S(2)}) async-start(bf16[8,16,896]{2,1,0:T(8,128)(2,1)} %broadcast_in_dim.89), calls=%async_computation.1 | async-start | bytes 458752 | tf_op jit(solution)/shard_map/all_to_all | solution.py:23
  40.0 3.3 %pack.1 = bf16[64,128,128]{2,1,0:T(8,128)(2,1)} custom-call(s32[64]{0:T(128)} %select_reduce_fusion.pick, s32[32]{0:T(128)} %get-tuple-element.9.at, bf16[32,1,64,128]{3,2,1,0:T(8,128)(2,1)} %keys.1, bf16[32,1,64,128]{3,2,1,0:T(8,128)(2,1)} %values.1, f32[32,128]{1,0:T(8,128)} %copy-done.8, f32[32,128]{1,0:T(8,128)} %copy-done.9), custom_call_target="tpu_custom_call" | custom-call | tf_op jit(solution)/shard_map/pack/pallas_call | solution.py:241
  43.3 4.4 %all-to-all-done.1 = bf16[8,16,896]{2,1,0:T(8,128)(2,1)S(1)} async-done(((bf16[8,16,896]{2,1,0:T(8,128)(2,1)}), bf16[8,16,896]{2,1,0:T(8,128)(2,1)S(1)}, u32[]{:S(2)}, u32[]{:S(2)}) %all-to-all-start.1) | async-done | bytes 229408 | tf_op jit(solution)/shard_map/all_to_all | solution.py:23
  47.6 5.7 %all-to-all-start.2 = ((bf16[64,128,128]{2,1,0:T(8,128)(2,1)}), bf16[64,128,128]{2,1,0:T(8,128)(2,1)}, u32[]{:S(2)}, u32[]{:S(2)}) async-start(bf16[64,128,128]{2,1,0:T(8,128)(2,1)} %pack.1), calls=%async_computation.2 | async-start | bytes 4194304 | tf_op jit(solution)/shard_map/all_to_all | solution.py:431
  54.0 0.9 collective-permute-start.2
  55.5 0.8 collective-permute-start.9
  56.6 1.1 collective-permute-done.2.other
  58.3 1.6 %collective-permute-start.5 = (bf16[64,896]{1,0:T(8,128)(2,1)}, bf16[64,896]{1,0:T(8,128)(2,1)S(1)}, u32[]{:S(2)}, u32[]{:S(2)}) collective-permute-start(bf16[64,896]{1,0:T(8,128)(2,1)} %after.3), channel_id=1, source_target_pairs={{192,0},{0,64},{64,128},{128,192},{193,1},{1,65},{65,129},{129,193... | collective-permute-start | bytes 344072 | tf_op jit(solution)/shard_map/ppermute | solution.py:17
  59.9 2.4 %collective-permute-start.4 = (bf16[64,896]{1,0:T(8,128)(2,1)}, bf16[64,896]{1,0:T(8,128)(2,1)S(1)}, u32[]{:S(2)}, u32[]{:S(2)}) collective-permute-start(bf16[64,896]{1,0:T(8,128)(2,1)} %after.3), channel_id=1, source_target_pairs={{128,0},{192,64},{0,128},{64,192},{129,1},{193,65},{1,129},{65,193... | collective-permute-start | bytes 344072 | tf_op jit(solution)/shard_map/ppermute | solution.py:17
  62.3 1.1 collective-permute-start.3
  63.5 1.0 pad_maximum_fusion.1.refs_4_
  64.9 5.0 %collective-permute-done.4 = bf16[64,896]{1,0:T(8,128)(2,1)S(1)} collective-permute-done((bf16[64,896]{1,0:T(8,128)(2,1)}, bf16[64,896]{1,0:T(8,128)(2,1)S(1)}, u32[]{:S(2)}, u32[]{:S(2)}) %collective-permute-start.4) | collective-permute-done | bytes 114720 | tf_op jit(solution)/shard_map/ppermute | solution.py:17
  70.9 2.2 %collective-permute-start.13 = (bf16[4,64,896]{2,1,0:T(8,128)(2,1)S(1)}, bf16[4,64,896]{2,1,0:T(8,128)(2,1)}, u32[]{:S(2)}, u32[]{:S(2)}) collective-permute-start(bf16[4,64,896]{2,1,0:T(8,128)(2,1)S(1)} %pad_maximum_fusion.1.refs_4_), channel_id=1, source_target_pairs={{192,0},{65,1},{0,64},{129,65},{64,128},{193,129},{128,192},{1,193... | collective-permute-start | bytes 1376264 | tf_op jit(solution)/shard_map/ppermute | solution.py:42
  73.1 2.4 %collective-permute-start.8 = (bf16[4,64,896]{2,1,0:T(8,128)(2,1)S(1)}, bf16[4,64,896]{2,1,0:T(8,128)(2,1)}, u32[]{:S(2)}, u32[]{:S(2)}) collective-permute-start(bf16[4,64,896]{2,1,0:T(8,128)(2,1)S(1)} %pad_maximum_fusion.refs_0_), channel_id=1, source_target_pairs={{6,0},{3,1},{0,2},{5,3},{2,4},{7,5},{4,6},{1,7},{14,8},{11,9},{8,1... | collective-permute-start | bytes 1376264 | tf_op jit(solution)/shard_map/ppermute | solution.py:42
  75.5 8.0 %collective-permute-done.11.refs_5_ = bf16[4,64,896]{2,1,0:T(8,128)(2,1)S(1)} collective-permute-done((bf16[4,64,896]{2,1,0:T(8,128)(2,1)S(1)}, bf16[4,64,896]{2,1,0:T(8,128)(2,1)S(1)}, u32[]{:S(2)}, u32[]{:S(2)}) %collective-permute-start.11) | collective-permute-done | bytes 458784 | tf_op jit(solution)/shard_map/ppermute | solution.py:42
  83.5 1.6 %collective-permute-start.7 = (bf16[4,64,896]{2,1,0:T(8,128)(2,1)}, bf16[4,64,896]{2,1,0:T(8,128)(2,1)}, u32[]{:S(2)}, u32[]{:S(2)}) collective-permute-start(bf16[4,64,896]{2,1,0:T(8,128)(2,1)} %collective-permute-done.6.refs_1_), channel_id=1, source_target_pairs={{2,0},{7,1},{4,2},{1,3},{6,4},{3,5},{0,6},{5,7},{10,8},{15,9},{12,... | collective-permute-start | bytes 1376264 | tf_op jit(solution)/shard_map/ppermute | solution.py:42
  86.6 0.8 reshape.310.refs_10_
  88.0 3.6 %collective-permute-done.13.refs_7_ = bf16[4,64,896]{2,1,0:T(8,128)(2,1)} collective-permute-done((bf16[4,64,896]{2,1,0:T(8,128)(2,1)S(1)}, bf16[4,64,896]{2,1,0:T(8,128)(2,1)}, u32[]{:S(2)}, u32[]{:S(2)}) %collective-permute-start.13) | collective-permute-done | bytes 458784 | tf_op jit(solution)/shard_map/ppermute | solution.py:42
  91.6 9.8 %collective-permute-done.12.refs_6_ = bf16[4,64,896]{2,1,0:T(8,128)(2,1)} collective-permute-done((bf16[4,64,896]{2,1,0:T(8,128)(2,1)S(1)}, bf16[4,64,896]{2,1,0:T(8,128)(2,1)}, u32[]{:S(2)}, u32[]{:S(2)}) %collective-permute-start.12) | collective-permute-done | bytes 458784 | tf_op jit(solution)/shard_map/ppermute | solution.py:42
  101.4 11.0 %head.1.value = f32[256,128]{1,0:T(8,128)} custom-call(s32[2,4]{1,0:T(2,128)} %pad_add_fusion.4.y_ref, bf16[4,64,896]{2,1,0:T(8,128)(2,1)} %copy-done.3, bf16[4,64,896]{2,1,0:T(8,128)(2,1)} %collective-permute-done.6.refs_1_, bf16[4,64,896]{2,1,0:T(8,128)(2,1)} %collective-permute-done.7.refs_2_, bf16[4,64,896]{2,1,0:T(8,128)(2,1)} %collective-permute-done.8.refs_3_, ...), custom_call_target="tpu_custom_call" | custom-call | tf_op jit(solution)/shard_map/head/pallas_call | solution.py:128
  112.5 12.2 %all-to-all-start.3 = ((f32[256,1,128]{2,1,0:T(1,128)}), f32[256,1,128]{2,1,0:T(1,128)S(1)}, u32[]{:S(2)}, u32[]{:S(2)}) async-start(f32[256,1,128]{2,1,0:T(1,128)} %bitcast.60), calls=%async_computation.3 | async-start | bytes 262144 | tf_op jit(solution)/shard_map/all_to_all | solution.py:434
  125.3 5.6 %settle.1 = (bf16[64,1,64,128]{3,2,1,0:T(8,128)(2,1)}, bf16[64,1,64,128]{3,2,1,0:T(8,128)(2,1)}) custom-call(bf16[64,128,128]{2,1,0:T(8,128)(2,1)} %all-to-all-done.2.other.got), custom_call_target="tpu_custom_call" | custom-call | tf_op jit(solution)/shard_map/settle/pallas_call | solution.py:261
  131.0 6.6 %all-to-all-done.3.value = f32[256,1,128]{2,1,0:T(1,128)S(1)} async-done(((f32[256,1,128]{2,1,0:T(1,128)}), f32[256,1,128]{2,1,0:T(1,128)S(1)}, u32[]{:S(2)}, u32[]{:S(2)}) %all-to-all-start.3) | async-done | bytes 131104 | tf_op jit(solution)/shard_map/all_to_all | solution.py:434
  138.3 1.2 reduce_max.29
  (125 shorter events, 18.0 us)
Async XLA Ops:
  0.6 17.4 %copy-start = (bf16[256,3584]{1,0:T(8,128)(2,1)S(1)}, bf16[256,3584]{1,0:T(8,128)(2,1)}, u32[]{:S(2)}) copy-start(bf16[256,3584]{1,0:T(8,128)(2,1)} %param.28) | copy-start | bytes 5505028
  0.7 13.4 %copy-start.1 = (bf16[32,1,64,128]{3,2,1,0:T(8,128)(2,1)S(1)}, bf16[32,1,64,128]{3,2,1,0:T(8,128)(2,1)}, u32[]{:S(2)}) copy-start(bf16[32,1,64,128]{3,2,1,0:T(8,128)(2,1)} %keys.1) | copy-start | bytes 1572868
  4.2 10.8 %copy-start.5 = (bf16[32,1,64,128]{3,2,1,0:T(8,128)(2,1)S(1)}, bf16[32,1,64,128]{3,2,1,0:T(8,128)(2,1)}, u32[]{:S(2)}) copy-start(bf16[32,1,64,128]{3,2,1,0:T(8,128)(2,1)} %values.1) | copy-start | bytes 1572868
  8.3 4.4 %collective-permute-start = (bf16[32,384]{1,0:T(8,128)(2,1)}, bf16[32,384]{1,0:T(8,128)(2,1)S(1)}, u32[]{:S(2)}, u32[]{:S(2)}) collective-permute-start(bf16[32,384]{1,0:T(8,128)(2,1)} %project.1), channel_id=1, source_target_pairs={{1,0},{0,1},{3,2},{2,3},{5,4},{4,5},{7,6},{6,7},{9,8},{8,9},{11,10... | collective-permute-start | bytes 73736 | tf_op jit(solution)/shard_map/ppermute | solution.py:17
  13.9 2.0 %copy-start.8 = (f32[32,128]{1,0:T(8,128)}, f32[32,128]{1,0:T(8,128)S(1)}, u32[]{:S(2)}) copy-start(f32[32,128]{1,0:T(8,128)S(1)} %maximum_convert_fusion.1.key_new) | copy-start | bytes 49156
  15.0 1.0 copy-start.9
  16.0 1.8 %collective-permute-start.1 = (f32[32,2,384]{0,1,2:T(2,128)S(1)}, f32[32,2,384]{0,1,2:T(2,128)S(1)}, u32[]{:S(2)}, u32[]{:S(2)}) collective-permute-start(f32[32,2,384]{0,1,2:T(2,128)S(1)} %bitcast.66), channel_id=1, source_target_pairs={{1,0},{0,1},{3,2},{2,3},{5,4},{4,5},{7,6},{6,7},{9,8},{8,9},{11,10... | collective-permute-start | bytes 294920 | tf_op jit(solution)/shard_map/ppermute | solution.py:17
  17.9 5.7 %copy-start.11 = (s32[1024,1]{0,1:T(1,128)S(1)}, s32[1024,1]{0,1:T(1,128)}, u32[]{:S(2)}) copy-start(s32[1024,1]{0,1:T(1,128)} %param.21) | copy-start | bytes 12292
  19.2 9.9 %all-to-all-start = ((bf16[8,16,896]{2,1,0:T(8,128)(2,1)}), bf16[8,16,896]{2,1,0:T(8,128)(2,1)S(1)}, u32[]{:S(2)}, u32[]{:S(2)}) async-start(bf16[8,16,896]{2,1,0:T(8,128)(2,1)} %bitcast.10), calls=%async_computation | async-start | bytes 458752 | tf_op jit(solution)/shard_map/all_to_all | solution.py:387
  22.9 78.5 %collective-permute-start.14 = (bf16[594,3584]{1,0:T(8,128)(2,1)}, bf16[594,3584]{1,0:T(8,128)(2,1)}, u32[]{:S(2)}, u32[]{:S(2)}) collective-permute-start(bf16[594,3584]{1,0:T(8,128)(2,1)} %refs_11_.1), channel_id=1, source_target_pairs={{1,0},{0,1},{3,2},{2,3},{5,4},{4,5},{7,6},{6,7},{9,8},{8,9},{11,10... | collective-permute-start | bytes 12773384 | tf_op jit(solution)/shard_map/ppermute | solution.py:17
  30.6 17.0 %all-to-all-start.1 = ((bf16[8,16,896]{2,1,0:T(8,128)(2,1)}), bf16[8,16,896]{2,1,0:T(8,128)(2,1)S(1)}, u32[]{:S(2)}, u32[]{:S(2)}) async-start(bf16[8,16,896]{2,1,0:T(8,128)(2,1)} %broadcast_in_dim.89), calls=%async_computation.1 | async-start | bytes 458752 | tf_op jit(solution)/shard_map/all_to_all | solution.py:23
  47.6 64.8 %all-to-all-start.2 = ((bf16[64,128,128]{2,1,0:T(8,128)(2,1)}), bf16[64,128,128]{2,1,0:T(8,128)(2,1)}, u32[]{:S(2)}, u32[]{:S(2)}) async-start(bf16[64,128,128]{2,1,0:T(8,128)(2,1)} %pack.1), calls=%async_computation.2 | async-start | bytes 4194304 | tf_op jit(solution)/shard_map/all_to_all | solution.py:431
  53.3 31.8 %copy-start.10 = (bf16[3584]{0:T(1024)(128)(2,1)S(1)}, bf16[3584]{0:T(1024)(128)(2,1)}, u32[]{:S(2)}) copy-start(bf16[3584]{0:T(1024)(128)(2,1)} %param.30) | copy-start | bytes 21508
  54.0 3.6 %collective-permute-start.2 = (bf16[64,896]{1,0:T(8,128)(2,1)S(1)}, bf16[64,896]{1,0:T(8,128)(2,1)S(1)}, u32[]{:S(2)}, u32[]{:S(2)}) collective-permute-start(bf16[64,896]{1,0:T(8,128)(2,1)S(1)} %get-tuple-element.22), channel_id=1, source_target_pairs={{2,0},{4,2},{6,4},{0,6},{3,1},{5,3},{7,5},{1,7},{10,8},{12,10},{14... | collective-permute-start | bytes 344072 | tf_op jit(solution)/shard_map/ppermute | solution.py:17
  54.9 7.4 %collective-permute-start.10 = (bf16[64,896]{1,0:T(8,128)(2,1)S(1)}, bf16[64,896]{1,0:T(8,128)(2,1)S(1)}, u32[]{:S(2)}, u32[]{:S(2)}) collective-permute-start(bf16[64,896]{1,0:T(8,128)(2,1)S(1)} %get-tuple-element.22), channel_id=1, source_target_pairs={{6,0},{0,2},{2,4},{4,6},{7,1},{1,3},{3,5},{5,7},{14,8},{8,10},{10,... | collective-permute-start | bytes 344072 | tf_op jit(solution)/shard_map/ppermute | solution.py:17
  55.5 8.0 %collective-permute-start.9 = (bf16[64,896]{1,0:T(8,128)(2,1)S(1)}, bf16[64,896]{1,0:T(8,128)(2,1)S(1)}, u32[]{:S(2)}, u32[]{:S(2)}) collective-permute-start(bf16[64,896]{1,0:T(8,128)(2,1)S(1)} %get-tuple-element.22), channel_id=1, source_target_pairs={{4,0},{6,2},{0,4},{2,6},{5,1},{7,3},{1,5},{3,7},{12,8},{14,10},{8,... | collective-permute-start | bytes 344072 | tf_op jit(solution)/shard_map/ppermute | solution.py:17
  57.7 0.6 copy-start.6
  58.3 6.5 %collective-permute-start.5 = (bf16[64,896]{1,0:T(8,128)(2,1)}, bf16[64,896]{1,0:T(8,128)(2,1)S(1)}, u32[]{:S(2)}, u32[]{:S(2)}) collective-permute-start(bf16[64,896]{1,0:T(8,128)(2,1)} %after.3), channel_id=1, source_target_pairs={{192,0},{0,64},{64,128},{128,192},{193,1},{1,65},{65,129},{129,193... | collective-permute-start | bytes 344072 | tf_op jit(solution)/shard_map/ppermute | solution.py:17
  59.9 10.0 %collective-permute-start.4 = (bf16[64,896]{1,0:T(8,128)(2,1)}, bf16[64,896]{1,0:T(8,128)(2,1)S(1)}, u32[]{:S(2)}, u32[]{:S(2)}) collective-permute-start(bf16[64,896]{1,0:T(8,128)(2,1)} %after.3), channel_id=1, source_target_pairs={{128,0},{192,64},{0,128},{64,192},{129,1},{193,65},{1,129},{65,193... | collective-permute-start | bytes 344072 | tf_op jit(solution)/shard_map/ppermute | solution.py:17
  62.3 7.5 %collective-permute-start.3 = (bf16[64,896]{1,0:T(8,128)(2,1)}, bf16[64,896]{1,0:T(8,128)(2,1)S(1)}, u32[]{:S(2)}, u32[]{:S(2)}) collective-permute-start(bf16[64,896]{1,0:T(8,128)(2,1)} %after.3), channel_id=1, source_target_pairs={{64,0},{128,64},{192,128},{0,192},{65,1},{129,65},{193,129},{1,193... | collective-permute-start | bytes 344072 | tf_op jit(solution)/shard_map/ppermute | solution.py:17
  64.5 36.9 %copy-start.2 = (bf16[4,64,896]{2,1,0:T(8,128)(2,1)}, bf16[4,64,896]{2,1,0:T(8,128)(2,1)S(1)}, u32[]{:S(2)}) copy-start(bf16[4,64,896]{2,1,0:T(8,128)(2,1)S(1)} %pad_maximum_fusion.1.refs_4_) | copy-start | bytes 1376260
  64.5 19.0 %collective-permute-start.11 = (bf16[4,64,896]{2,1,0:T(8,128)(2,1)S(1)}, bf16[4,64,896]{2,1,0:T(8,128)(2,1)S(1)}, u32[]{:S(2)}, u32[]{:S(2)}) collective-permute-start(bf16[4,64,896]{2,1,0:T(8,128)(2,1)S(1)} %pad_maximum_fusion.1.refs_4_), channel_id=1, source_target_pairs={{64,0},{193,1},{128,64},{1,65},{192,128},{65,129},{0,192},{129,193... | collective-permute-start | bytes 1376264 | tf_op jit(solution)/shard_map/ppermute | solution.py:42
  70.0 31.4 %copy-start.3 = (bf16[4,64,896]{2,1,0:T(8,128)(2,1)}, bf16[4,64,896]{2,1,0:T(8,128)(2,1)S(1)}, u32[]{:S(2)}) copy-start(bf16[4,64,896]{2,1,0:T(8,128)(2,1)S(1)} %pad_maximum_fusion.refs_0_) | copy-start | bytes 1376260
  70.0 13.6 %collective-permute-start.6 = (bf16[4,64,896]{2,1,0:T(8,128)(2,1)S(1)}, bf16[4,64,896]{2,1,0:T(8,128)(2,1)}, u32[]{:S(2)}, u32[]{:S(2)}) collective-permute-start(bf16[4,64,896]{2,1,0:T(8,128)(2,1)S(1)} %pad_maximum_fusion.refs_0_), channel_id=1, source_target_pairs={{2,0},{7,1},{4,2},{1,3},{6,4},{3,5},{0,6},{5,7},{10,8},{15,9},{12,... | collective-permute-start | bytes 1376264 | tf_op jit(solution)/shard_map/ppermute | solution.py:42
  70.9 20.7 %collective-permute-start.13 = (bf16[4,64,896]{2,1,0:T(8,128)(2,1)S(1)}, bf16[4,64,896]{2,1,0:T(8,128)(2,1)}, u32[]{:S(2)}, u32[]{:S(2)}) collective-permute-start(bf16[4,64,896]{2,1,0:T(8,128)(2,1)S(1)} %pad_maximum_fusion.1.refs_4_), channel_id=1, source_target_pairs={{192,0},{65,1},{0,64},{129,65},{64,128},{193,129},{128,192},{1,193... | collective-permute-start | bytes 1376264 | tf_op jit(solution)/shard_map/ppermute | solution.py:42
  73.1 18.5 %collective-permute-start.8 = (bf16[4,64,896]{2,1,0:T(8,128)(2,1)S(1)}, bf16[4,64,896]{2,1,0:T(8,128)(2,1)}, u32[]{:S(2)}, u32[]{:S(2)}) collective-permute-start(bf16[4,64,896]{2,1,0:T(8,128)(2,1)S(1)} %pad_maximum_fusion.refs_0_), channel_id=1, source_target_pairs={{6,0},{3,1},{0,2},{5,3},{2,4},{7,5},{4,6},{1,7},{14,8},{11,9},{8,1... | collective-permute-start | bytes 1376264 | tf_op jit(solution)/shard_map/ppermute | solution.py:42
  83.5 17.9 %copy-start.7 = (bf16[4,64,896]{2,1,0:T(8,128)(2,1)}, bf16[4,64,896]{2,1,0:T(8,128)(2,1)S(1)}, u32[]{:S(2)}) copy-start(bf16[4,64,896]{2,1,0:T(8,128)(2,1)S(1)} %collective-permute-done.11.refs_5_) | copy-start | bytes 1376260
  83.5 17.9 %collective-permute-start.12 = (bf16[4,64,896]{2,1,0:T(8,128)(2,1)S(1)}, bf16[4,64,896]{2,1,0:T(8,128)(2,1)}, u32[]{:S(2)}, u32[]{:S(2)}) collective-permute-start(bf16[4,64,896]{2,1,0:T(8,128)(2,1)S(1)} %collective-permute-done.11.refs_5_), channel_id=1, source_target_pairs={{64,0},{193,1},{128,64},{1,65},{192,128},{65,129},{0,192},{129,193... | collective-permute-start | bytes 1376264 | tf_op jit(solution)/shard_map/ppermute | solution.py:42
  83.5 17.9 %collective-permute-start.7 = (bf16[4,64,896]{2,1,0:T(8,128)(2,1)}, bf16[4,64,896]{2,1,0:T(8,128)(2,1)}, u32[]{:S(2)}, u32[]{:S(2)}) collective-permute-start(bf16[4,64,896]{2,1,0:T(8,128)(2,1)} %collective-permute-done.6.refs_1_), channel_id=1, source_target_pairs={{2,0},{7,1},{4,2},{1,3},{6,4},{3,5},{0,6},{5,7},{10,8},{15,9},{12,... | collective-permute-start | bytes 1376264 | tf_op jit(solution)/shard_map/ppermute | solution.py:42
  112.5 25.1 %all-to-all-start.3 = ((f32[256,1,128]{2,1,0:T(1,128)}), f32[256,1,128]{2,1,0:T(1,128)S(1)}, u32[]{:S(2)}, u32[]{:S(2)}) async-start(f32[256,1,128]{2,1,0:T(1,128)} %bitcast.60), calls=%async_computation.3 | async-start | bytes 262144 | tf_op jit(solution)/shard_map/all_to_all | solution.py:434
  137.6 0.6 copy-start.4

commit v4 on v3

--- a/solution.py
+++ b/solution.py
@@ -395,6 +395,7 @@
     part_a = by_z[:, :part].reshape(n_z * part, cols)
     from_y = [part_b] + [shifted(part_b, "y", d) for d in range(1, n_y)]
     late_a = after(part_a, from_y[1])
+    send_kv = after(send_kv, from_y[1])
     from_x = [part_a] + [shifted(late_a, "x", d) for d in range(1, n_x)]
     by_z = after(by_z, send_kv)
     block_b = jnp.stack(from_y)

time: 141 us -> 146 us (1.035)
  starting transfers between devices: 47.8 us -> 51.6 us
  waiting for transfers between devices: 45.6 us -> 47.7 us
    ppermute x9, starting transfers between devices: 11.4 us -> 14 us  [shifted(): lax.ppermute(value, axis, [((i + distance) % size, i) for i in range(size)])]
    ppermute x6, waiting for transfers between devices: 21.4 us -> 19.5 us  [from_side(): return lax.ppermute(value, (axis, 'c'), pairs)]
    all_to_all x1, waiting for transfers between devices: 4.36 us -> 5.94 us  [spread(): return lax.all_to_all(copies, axis, split_axis=0, concat_axis=0, tiled=True)]
  transfers between devices with their start and end apart: 19 -> 19, of which waited for: 10 -> 11; matrix products, arithmetic and copies ran while one was open for 7% -> 5% of each run, Pallas kernels for 14% -> 14%
where the time goes in v4:
time: 146 us; the launch traced here: 145 us
  starting transfers between devices  51.6 us (35%)
  waiting for transfers between devices  47.7 us (33%)
  Pallas kernels  24.1 us (17%)
  other arithmetic  11 us (8%)
  local copies, waits for them, and re-layouts  8.3 us (6%)
    ppermute x6, waiting for transfers between devices, from_side(): return lax.ppermute(value, (axis, 'c'), pairs)  19.5 us
    ppermute x9, starting transfers between devices, shifted(): lax.ppermute(value, axis, [((i + distance) % size, i) for i in range(size)])  14 us
    all_to_all x1, starting transfers between devices, per_device(): arrived = lax.all_to_all(send, ALL, split_axis=0, concat_axis=0, tiled=True)  12 us
    pallas_call x1, Pallas kernels, head(): pl.pallas_call(head_kernel, in_specs=[pl.BlockSpec(memory_space=pltpu.SME...  11.1 us
    ppermute x9, waiting for transfers between devices, shifted(): lax.ppermute(value, axis, [((i + distance) % size, i) for i in range(size)])  9.37 us
    ppermute x6, starting transfers between devices, from_side(): return lax.ppermute(value, (axis, 'c'), pairs)  8.62 us
    all_to_all x1, starting transfers between devices, spread(): return lax.all_to_all(copies, axis, split_axis=0, concat_axis=0, tiled=True)  7.59 us
    all_to_all x1, waiting for transfers between devices, per_device(): arrived = lax.all_to_all(send, ALL, split_axis=0, concat_axis=0, tiled=True)  6.63 us
  transfers between devices with their start and end apart: 19, of which 11 were waited for; matrix products, arithmetic and copies ran while one was open for 5% of the time, Pallas kernels for 14%

profile of v4, /device:TPU:1, one launch (start us, length us, event | category | flops | bytes accessed | tf_op | source)
XLA Modules:
  0.0 145.1 jit_solution(6825285195641962707)
XLA Ops:
  0.7 1.4 broadcast_subtract_fusion
  2.9 1.3 maximum_bitcast_fusion.bias
  4.2 4.1 %project.1 = bf16[32,384]{1,0:T(8,128)(2,1)} custom-call(bf16[32,3584]{1,0:T(8,128)(2,1)} %x_ref.1, bf16[28,128]{1,0:T(8,128)(2,1)} %bitcast.75, bf16[3,128]{1,0:T(4,128)(2,1)} %maximum_bitcast_fusion.bias, f32[32,64]{1,0:T(8,128)} %get-tuple-element.41.cos, f32[32,64]{1,0:T(8,128)} %get-tuple-element.40.sin, bf16[3584,256]{1,0:T(8,128)(2,1)} %wq_ref.1, ...), custom_call_target="tpu_custom_call" | custom-call | tf_op jit(solution)/shard_map/project/pallas_call | solution.py:207
  8.3 3.3 %collective-permute-start = (bf16[32,384]{1,0:T(8,128)(2,1)}, bf16[32,384]{1,0:T(8,128)(2,1)S(1)}, u32[]{:S(2)}, u32[]{:S(2)}) collective-permute-start(bf16[32,384]{1,0:T(8,128)(2,1)} %project.1), channel_id=1, source_target_pairs={{1,0},{0,1},{3,2},{2,3},{5,4},{4,5},{7,6},{6,7},{9,8},{8,9},{11,10... | collective-permute-start | bytes 73736 | tf_op jit(solution)/shard_map/ppermute | solution.py:17
  11.7 1.0 collective-permute-done
  16.4 1.4 collective-permute-done.1
  19.2 3.7 %all-to-all-start = ((bf16[8,16,896]{2,1,0:T(8,128)(2,1)}), bf16[8,16,896]{2,1,0:T(8,128)(2,1)S(1)}, u32[]{:S(2)}, u32[]{:S(2)}) async-start(bf16[8,16,896]{2,1,0:T(8,128)(2,1)} %bitcast.10), calls=%async_computation | async-start | bytes 458752 | tf_op jit(solution)/shard_map/all_to_all | solution.py:387
  22.9 6.2 %all-to-all-done = bf16[8,16,896]{2,1,0:T(8,128)(2,1)S(1)} async-done(((bf16[8,16,896]{2,1,0:T(8,128)(2,1)}), bf16[8,16,896]{2,1,0:T(8,128)(2,1)S(1)}, u32[]{:S(2)}, u32[]{:S(2)}) %all-to-all-start) | async-done | bytes 229408 | tf_op jit(solution)/shard_map/all_to_all | solution.py:387
  30.6 7.6 %all-to-all-start.1 = ((bf16[8,16,896]{2,1,0:T(8,128)(2,1)}), bf16[8,16,896]{2,1,0:T(8,128)(2,1)S(1)}, u32[]{:S(2)}, u32[]{:S(2)}) async-start(bf16[8,16,896]{2,1,0:T(8,128)(2,1)} %broadcast_in_dim.89), calls=%async_computation.1 | async-start | bytes 458752 | tf_op jit(solution)/shard_map/all_to_all | solution.py:23
  38.2 1.3 collective-permute-start.14
  41.7 5.9 %all-to-all-done.1 = bf16[8,16,896]{2,1,0:T(8,128)(2,1)S(1)} async-done(((bf16[8,16,896]{2,1,0:T(8,128)(2,1)}), bf16[8,16,896]{2,1,0:T(8,128)(2,1)S(1)}, u32[]{:S(2)}, u32[]{:S(2)}) %all-to-all-start.1) | async-done | bytes 229408 | tf_op jit(solution)/shard_map/all_to_all | solution.py:23
  48.3 0.9 collective-permute-start.2
  50.0 3.3 %pack.1.value = bf16[64,128,128]{2,1,0:T(8,128)(2,1)} custom-call(s32[64]{0:T(128)} %select_reduce_fusion.pick, s32[32]{0:T(128)} %get-tuple-element.9.at, bf16[32,1,64,128]{3,2,1,0:T(8,128)(2,1)} %keys.1, bf16[32,1,64,128]{3,2,1,0:T(8,128)(2,1)} %values.1, f32[32,128]{1,0:T(8,128)} %copy-done.9, f32[32,128]{1,0:T(8,128)} %copy-done.10), custom_call_target="tpu_custom_call" | custom-call | tf_op jit(solution)/shard_map/pack/pallas_call | solution.py:241
  53.9 5.8 %all-to-all-start.2 = ((bf16[64,128,128]{2,1,0:T(8,128)(2,1)}), bf16[64,128,128]{2,1,0:T(8,128)(2,1)}, u32[]{:S(2)}, u32[]{:S(2)}) async-start(bf16[64,128,128]{2,1,0:T(8,128)(2,1)} %after.5), calls=%async_computation.2 | async-start | bytes 4194304 | tf_op jit(solution)/shard_map/all_to_all | solution.py:432
  60.5 1.3 collective-permute-start.9
  62.1 1.2 collective-permute-start.5
  63.3 2.4 %collective-permute-start.4 = (bf16[64,896]{1,0:T(8,128)(2,1)}, bf16[64,896]{1,0:T(8,128)(2,1)S(1)}, u32[]{:S(2)}, u32[]{:S(2)}) collective-permute-start(bf16[64,896]{1,0:T(8,128)(2,1)} %after.4), channel_id=1, source_target_pairs={{128,0},{192,64},{0,128},{64,192},{129,1},{193,65},{1,129},{65,193... | collective-permute-start | bytes 344072 | tf_op jit(solution)/shard_map/ppermute | solution.py:17
  66.4 2.4 %collective-permute-start.3 = (bf16[64,896]{1,0:T(8,128)(2,1)}, bf16[64,896]{1,0:T(8,128)(2,1)S(1)}, u32[]{:S(2)}, u32[]{:S(2)}) collective-permute-start(bf16[64,896]{1,0:T(8,128)(2,1)} %after.4), channel_id=1, source_target_pairs={{64,0},{128,64},{192,128},{0,192},{65,1},{129,65},{193,129},{1,193... | collective-permute-start | bytes 344072 | tf_op jit(solution)/shard_map/ppermute | solution.py:17
  68.9 1.4 collective-permute-done.5
  70.3 5.0 %collective-permute-done.4 = bf16[64,896]{1,0:T(8,128)(2,1)S(1)} collective-permute-done((bf16[64,896]{1,0:T(8,128)(2,1)}, bf16[64,896]{1,0:T(8,128)(2,1)S(1)}, u32[]{:S(2)}, u32[]{:S(2)}) %collective-permute-start.4) | collective-permute-done | bytes 114720 | tf_op jit(solution)/shard_map/ppermute | solution.py:17
  75.4 0.8 collective-permute-start.6
  76.5 4.5 %collective-permute-start.13 = (bf16[4,64,896]{2,1,0:T(8,128)(2,1)S(1)}, bf16[4,64,896]{2,1,0:T(8,128)(2,1)}, u32[]{:S(2)}, u32[]{:S(2)}) collective-permute-start(bf16[4,64,896]{2,1,0:T(8,128)(2,1)S(1)} %pad_maximum_fusion.1.refs_4_), channel_id=1, source_target_pairs={{192,0},{65,1},{0,64},{129,65},{64,128},{193,129},{128,192},{1,193... | collective-permute-start | bytes 1376264 | tf_op jit(solution)/shard_map/ppermute | solution.py:42
  80.9 2.7 %collective-permute-start.8 = (bf16[4,64,896]{2,1,0:T(8,128)(2,1)S(1)}, bf16[4,64,896]{2,1,0:T(8,128)(2,1)}, u32[]{:S(2)}, u32[]{:S(2)}) collective-permute-start(bf16[4,64,896]{2,1,0:T(8,128)(2,1)S(1)} %pad_maximum_fusion.refs_0_), channel_id=1, source_target_pairs={{6,0},{3,1},{0,2},{5,3},{2,4},{7,5},{4,6},{1,7},{14,8},{11,9},{8,1... | collective-permute-start | bytes 1376264 | tf_op jit(solution)/shard_map/ppermute | solution.py:42
  83.6 2.6 %collective-permute-done.11.refs_5_ = bf16[4,64,896]{2,1,0:T(8,128)(2,1)S(1)} collective-permute-done((bf16[4,64,896]{2,1,0:T(8,128)(2,1)S(1)}, bf16[4,64,896]{2,1,0:T(8,128)(2,1)S(1)}, u32[]{:S(2)}, u32[]{:S(2)}) %collective-permute-start.11) | collective-permute-done | bytes 458784 | tf_op jit(solution)/shard_map/ppermute | solution.py:42
  88.3 0.8 reshape.310.refs_10_
  89.8 5.4 %collective-permute-done.13.refs_7_ = bf16[4,64,896]{2,1,0:T(8,128)(2,1)} collective-permute-done((bf16[4,64,896]{2,1,0:T(8,128)(2,1)S(1)}, bf16[4,64,896]{2,1,0:T(8,128)(2,1)}, u32[]{:S(2)}, u32[]{:S(2)}) %collective-permute-start.13) | collective-permute-done | bytes 458784 | tf_op jit(solution)/shard_map/ppermute | solution.py:42
  95.2 11.5 %collective-permute-done.12.refs_6_ = bf16[4,64,896]{2,1,0:T(8,128)(2,1)} collective-permute-done((bf16[4,64,896]{2,1,0:T(8,128)(2,1)S(1)}, bf16[4,64,896]{2,1,0:T(8,128)(2,1)}, u32[]{:S(2)}, u32[]{:S(2)}) %collective-permute-start.12) | collective-permute-done | bytes 458784 | tf_op jit(solution)/shard_map/ppermute | solution.py:42
  106.7 11.1 %head.1.value = f32[256,128]{1,0:T(8,128)} custom-call(s32[2,4]{1,0:T(2,128)} %pad_add_fusion.4.y_ref, bf16[4,64,896]{2,1,0:T(8,128)(2,1)} %copy-done.3, bf16[4,64,896]{2,1,0:T(8,128)(2,1)} %collective-permute-done.6.refs_1_, bf16[4,64,896]{2,1,0:T(8,128)(2,1)} %collective-permute-done.7.refs_2_, bf16[4,64,896]{2,1,0:T(8,128)(2,1)} %collective-permute-done.8.refs_3_, ...), custom_call_target="tpu_custom_call" | custom-call | tf_op jit(solution)/shard_map/head/pallas_call | solution.py:128
  117.8 12.0 %all-to-all-start.3 = ((f32[256,1,128]{2,1,0:T(1,128)}), f32[256,1,128]{2,1,0:T(1,128)S(1)}, u32[]{:S(2)}, u32[]{:S(2)}) async-start(f32[256,1,128]{2,1,0:T(1,128)} %bitcast.60), calls=%async_computation.3 | async-start | bytes 262144 | tf_op jit(solution)/shard_map/all_to_all | solution.py:435
  130.3 5.6 %settle.1 = (bf16[64,1,64,128]{3,2,1,0:T(8,128)(2,1)}, bf16[64,1,64,128]{3,2,1,0:T(8,128)(2,1)}) custom-call(bf16[64,128,128]{2,1,0:T(8,128)(2,1)} %all-to-all-done.2.other.got), custom_call_target="tpu_custom_call" | custom-call | tf_op jit(solution)/shard_map/settle/pallas_call | solution.py:261
  136.0 6.6 %all-to-all-done.3.value = f32[256,1,128]{2,1,0:T(1,128)S(1)} async-done(((f32[256,1,128]{2,1,0:T(1,128)}), f32[256,1,128]{2,1,0:T(1,128)S(1)}, u32[]{:S(2)}, u32[]{:S(2)}) %all-to-all-start.3) | async-done | bytes 131104 | tf_op jit(solution)/shard_map/all_to_all | solution.py:435
  143.3 1.2 reduce_max.29
  (128 shorter events, 18.1 us)
Async XLA Ops:
  0.6 17.4 %copy-start = (bf16[256,3584]{1,0:T(8,128)(2,1)S(1)}, bf16[256,3584]{1,0:T(8,128)(2,1)}, u32[]{:S(2)}) copy-start(bf16[256,3584]{1,0:T(8,128)(2,1)} %param.28) | copy-start | bytes 5505028
  0.6 13.4 %copy-start.1 = (bf16[32,1,64,128]{3,2,1,0:T(8,128)(2,1)S(1)}, bf16[32,1,64,128]{3,2,1,0:T(8,128)(2,1)}, u32[]{:S(2)}) copy-start(bf16[32,1,64,128]{3,2,1,0:T(8,128)(2,1)} %keys.1) | copy-start | bytes 1572868
  4.2 10.8 %copy-start.7 = (bf16[32,1,64,128]{3,2,1,0:T(8,128)(2,1)S(1)}, bf16[32,1,64,128]{3,2,1,0:T(8,128)(2,1)}, u32[]{:S(2)}) copy-start(bf16[32,1,64,128]{3,2,1,0:T(8,128)(2,1)} %values.1) | copy-start | bytes 1572868
  8.3 4.4 %collective-permute-start = (bf16[32,384]{1,0:T(8,128)(2,1)}, bf16[32,384]{1,0:T(8,128)(2,1)S(1)}, u32[]{:S(2)}, u32[]{:S(2)}) collective-permute-start(bf16[32,384]{1,0:T(8,128)(2,1)} %project.1), channel_id=1, source_target_pairs={{1,0},{0,1},{3,2},{2,3},{5,4},{4,5},{7,6},{6,7},{9,8},{8,9},{11,10... | collective-permute-start | bytes 73736 | tf_op jit(solution)/shard_map/ppermute | solution.py:17
  13.9 2.1 %copy-start.9 = (f32[32,128]{1,0:T(8,128)}, f32[32,128]{1,0:T(8,128)S(1)}, u32[]{:S(2)}) copy-start(f32[32,128]{1,0:T(8,128)S(1)} %maximum_convert_fusion.1.key_new) | copy-start | bytes 49156
  14.9 1.0 copy-start.10
  16.0 1.8 %collective-permute-start.1 = (f32[32,2,384]{0,1,2:T(2,128)S(1)}, f32[32,2,384]{0,1,2:T(2,128)S(1)}, u32[]{:S(2)}, u32[]{:S(2)}) collective-permute-start(f32[32,2,384]{0,1,2:T(2,128)S(1)} %bitcast.66), channel_id=1, source_target_pairs={{1,0},{0,1},{3,2},{2,3},{5,4},{4,5},{7,6},{6,7},{9,8},{8,9},{11,10... | collective-permute-start | bytes 294920 | tf_op jit(solution)/shard_map/ppermute | solution.py:17
  18.0 22.0 %copy-start.12 = (s32[1024,1]{0,1:T(1,128)S(1)}, s32[1024,1]{0,1:T(1,128)}, u32[]{:S(2)}) copy-start(s32[1024,1]{0,1:T(1,128)} %param.21) | copy-start | bytes 12292
  19.2 9.9 %all-to-all-start = ((bf16[8,16,896]{2,1,0:T(8,128)(2,1)}), bf16[8,16,896]{2,1,0:T(8,128)(2,1)S(1)}, u32[]{:S(2)}, u32[]{:S(2)}) async-start(bf16[8,16,896]{2,1,0:T(8,128)(2,1)} %bitcast.10), calls=%async_computation | async-start | bytes 458752 | tf_op jit(solution)/shard_map/all_to_all | solution.py:387
  30.6 17.0 %all-to-all-start.1 = ((bf16[8,16,896]{2,1,0:T(8,128)(2,1)}), bf16[8,16,896]{2,1,0:T(8,128)(2,1)S(1)}, u32[]{:S(2)}, u32[]{:S(2)}) async-start(bf16[8,16,896]{2,1,0:T(8,128)(2,1)} %broadcast_in_dim.89), calls=%async_computation.1 | async-start | bytes 458752 | tf_op jit(solution)/shard_map/all_to_all | solution.py:23
  38.2 68.5 %collective-permute-start.14 = (bf16[594,3584]{1,0:T(8,128)(2,1)}, bf16[594,3584]{1,0:T(8,128)(2,1)}, u32[]{:S(2)}, u32[]{:S(2)}) collective-permute-start(bf16[594,3584]{1,0:T(8,128)(2,1)} %refs_11_.1), channel_id=1, source_target_pairs={{1,0},{0,1},{3,2},{2,3},{5,4},{4,5},{7,6},{6,7},{9,8},{8,9},{11,10... | collective-permute-start | bytes 12773384 | tf_op jit(solution)/shard_map/ppermute | solution.py:17
  48.3 5.0 %collective-permute-start.2 = (bf16[64,896]{1,0:T(8,128)(2,1)S(1)}, bf16[64,896]{1,0:T(8,128)(2,1)S(1)}, u32[]{:S(2)}, u32[]{:S(2)}) collective-permute-start(bf16[64,896]{1,0:T(8,128)(2,1)S(1)} %get-tuple-element.22), channel_id=1, source_target_pairs={{2,0},{4,2},{6,4},{0,6},{3,1},{5,3},{7,5},{1,7},{10,8},{12,10},{14... | collective-permute-start | bytes 344072 | tf_op jit(solution)/shard_map/ppermute | solution.py:17
  53.3 0.6 copy-start.5
  53.9 14.8 %copy-start.6 = (bf16[64,896]{1,0:T(8,128)(2,1)S(1)}, bf16[64,896]{1,0:T(8,128)(2,1)}, u32[]{:S(2)}) copy-start(bf16[64,896]{1,0:T(8,128)(2,1)} %copy-done.5) | copy-start | bytes 344068
  53.9 63.8 %all-to-all-start.2 = ((bf16[64,128,128]{2,1,0:T(8,128)(2,1)}), bf16[64,128,128]{2,1,0:T(8,128)(2,1)}, u32[]{:S(2)}, u32[]{:S(2)}) async-start(bf16[64,128,128]{2,1,0:T(8,128)(2,1)} %after.5), calls=%async_computation.2 | async-start | bytes 4194304 | tf_op jit(solution)/shard_map/all_to_all | solution.py:432
  59.8 27.1 %copy-start.11 = (bf16[3584]{0:T(1024)(128)(2,1)S(1)}, bf16[3584]{0:T(1024)(128)(2,1)}, u32[]{:S(2)}) copy-start(bf16[3584]{0:T(1024)(128)(2,1)} %param.30) | copy-start | bytes 21508
  59.8 6.6 %collective-permute-start.10 = (bf16[64,896]{1,0:T(8,128)(2,1)S(1)}, bf16[64,896]{1,0:T(8,128)(2,1)S(1)}, u32[]{:S(2)}, u32[]{:S(2)}) collective-permute-start(bf16[64,896]{1,0:T(8,128)(2,1)S(1)} %get-tuple-element.22), channel_id=1, source_target_pairs={{6,0},{0,2},{2,4},{4,6},{7,1},{1,3},{3,5},{5,7},{14,8},{8,10},{10,... | collective-permute-start | bytes 344072 | tf_op jit(solution)/shard_map/ppermute | solution.py:17
  60.5 8.3 %collective-permute-start.9 = (bf16[64,896]{1,0:T(8,128)(2,1)S(1)}, bf16[64,896]{1,0:T(8,128)(2,1)S(1)}, u32[]{:S(2)}, u32[]{:S(2)}) collective-permute-start(bf16[64,896]{1,0:T(8,128)(2,1)S(1)} %get-tuple-element.22), channel_id=1, source_target_pairs={{4,0},{6,2},{0,4},{2,6},{5,1},{7,3},{1,5},{3,7},{12,8},{14,10},{8,... | collective-permute-start | bytes 344072 | tf_op jit(solution)/shard_map/ppermute | solution.py:17
  62.1 8.2 %collective-permute-start.5 = (bf16[64,896]{1,0:T(8,128)(2,1)}, bf16[64,896]{1,0:T(8,128)(2,1)S(1)}, u32[]{:S(2)}, u32[]{:S(2)}) collective-permute-start(bf16[64,896]{1,0:T(8,128)(2,1)} %after.4), channel_id=1, source_target_pairs={{192,0},{0,64},{64,128},{128,192},{193,1},{1,65},{65,129},{129,193... | collective-permute-start | bytes 344072 | tf_op jit(solution)/shard_map/ppermute | solution.py:17
  63.3 12.0 %collective-permute-start.4 = (bf16[64,896]{1,0:T(8,128)(2,1)}, bf16[64,896]{1,0:T(8,128)(2,1)S(1)}, u32[]{:S(2)}, u32[]{:S(2)}) collective-permute-start(bf16[64,896]{1,0:T(8,128)(2,1)} %after.4), channel_id=1, source_target_pairs={{128,0},{192,64},{0,128},{64,192},{129,1},{193,65},{1,129},{65,193... | collective-permute-start | bytes 344072 | tf_op jit(solution)/shard_map/ppermute | solution.py:17
  66.4 8.9 %collective-permute-start.3 = (bf16[64,896]{1,0:T(8,128)(2,1)}, bf16[64,896]{1,0:T(8,128)(2,1)S(1)}, u32[]{:S(2)}, u32[]{:S(2)}) collective-permute-start(bf16[64,896]{1,0:T(8,128)(2,1)} %after.4), channel_id=1, source_target_pairs={{64,0},{128,64},{192,128},{0,192},{65,1},{129,65},{193,129},{1,193... | collective-permute-start | bytes 344072 | tf_op jit(solution)/shard_map/ppermute | solution.py:17
  68.8 37.9 %copy-start.2 = (bf16[4,64,896]{2,1,0:T(8,128)(2,1)}, bf16[4,64,896]{2,1,0:T(8,128)(2,1)S(1)}, u32[]{:S(2)}) copy-start(bf16[4,64,896]{2,1,0:T(8,128)(2,1)S(1)} %pad_maximum_fusion.1.refs_4_) | copy-start | bytes 1376260
  68.8 17.4 %collective-permute-start.11 = (bf16[4,64,896]{2,1,0:T(8,128)(2,1)S(1)}, bf16[4,64,896]{2,1,0:T(8,128)(2,1)S(1)}, u32[]{:S(2)}, u32[]{:S(2)}) collective-permute-start(bf16[4,64,896]{2,1,0:T(8,128)(2,1)S(1)} %pad_maximum_fusion.1.refs_4_), channel_id=1, source_target_pairs={{64,0},{193,1},{128,64},{1,65},{192,128},{65,129},{0,192},{129,193... | collective-permute-start | bytes 1376264 | tf_op jit(solution)/shard_map/ppermute | solution.py:42
  75.4 31.3 %copy-start.3 = (bf16[4,64,896]{2,1,0:T(8,128)(2,1)}, bf16[4,64,896]{2,1,0:T(8,128)(2,1)S(1)}, u32[]{:S(2)}) copy-start(bf16[4,64,896]{2,1,0:T(8,128)(2,1)S(1)} %pad_maximum_fusion.refs_0_) | copy-start | bytes 1376260
  75.4 10.9 %collective-permute-start.6 = (bf16[4,64,896]{2,1,0:T(8,128)(2,1)S(1)}, bf16[4,64,896]{2,1,0:T(8,128)(2,1)}, u32[]{:S(2)}, u32[]{:S(2)}) collective-permute-start(bf16[4,64,896]{2,1,0:T(8,128)(2,1)S(1)} %pad_maximum_fusion.refs_0_), channel_id=1, source_target_pairs={{2,0},{7,1},{4,2},{1,3},{6,4},{3,5},{0,6},{5,7},{10,8},{15,9},{12,... | collective-permute-start | bytes 1376264 | tf_op jit(solution)/shard_map/ppermute | solution.py:42
  76.5 18.7 %collective-permute-start.13 = (bf16[4,64,896]{2,1,0:T(8,128)(2,1)S(1)}, bf16[4,64,896]{2,1,0:T(8,128)(2,1)}, u32[]{:S(2)}, u32[]{:S(2)}) collective-permute-start(bf16[4,64,896]{2,1,0:T(8,128)(2,1)S(1)} %pad_maximum_fusion.1.refs_4_), channel_id=1, source_target_pairs={{192,0},{65,1},{0,64},{129,65},{64,128},{193,129},{128,192},{1,193... | collective-permute-start | bytes 1376264 | tf_op jit(solution)/shard_map/ppermute | solution.py:42
  80.9 14.3 %collective-permute-start.8 = (bf16[4,64,896]{2,1,0:T(8,128)(2,1)S(1)}, bf16[4,64,896]{2,1,0:T(8,128)(2,1)}, u32[]{:S(2)}, u32[]{:S(2)}) collective-permute-start(bf16[4,64,896]{2,1,0:T(8,128)(2,1)S(1)} %pad_maximum_fusion.refs_0_), channel_id=1, source_target_pairs={{6,0},{3,1},{0,2},{5,3},{2,4},{7,5},{4,6},{1,7},{14,8},{11,9},{8,1... | collective-permute-start | bytes 1376264 | tf_op jit(solution)/shard_map/ppermute | solution.py:42
  86.2 20.5 %copy-start.8 = (bf16[4,64,896]{2,1,0:T(8,128)(2,1)}, bf16[4,64,896]{2,1,0:T(8,128)(2,1)S(1)}, u32[]{:S(2)}) copy-start(bf16[4,64,896]{2,1,0:T(8,128)(2,1)S(1)} %collective-permute-done.11.refs_5_) | copy-start | bytes 1376260
  86.2 20.4 %collective-permute-start.12 = (bf16[4,64,896]{2,1,0:T(8,128)(2,1)S(1)}, bf16[4,64,896]{2,1,0:T(8,128)(2,1)}, u32[]{:S(2)}, u32[]{:S(2)}) collective-permute-start(bf16[4,64,896]{2,1,0:T(8,128)(2,1)S(1)} %collective-permute-done.11.refs_5_), channel_id=1, source_target_pairs={{64,0},{193,1},{128,64},{1,65},{192,128},{65,129},{0,192},{129,193... | collective-permute-start | bytes 1376264 | tf_op jit(solution)/shard_map/ppermute | solution.py:42
  86.2 20.4 %collective-permute-start.7 = (bf16[4,64,896]{2,1,0:T(8,128)(2,1)}, bf16[4,64,896]{2,1,0:T(8,128)(2,1)}, u32[]{:S(2)}, u32[]{:S(2)}) collective-permute-start(bf16[4,64,896]{2,1,0:T(8,128)(2,1)} %collective-permute-done.6.refs_1_), channel_id=1, source_target_pairs={{2,0},{7,1},{4,2},{1,3},{6,4},{3,5},{0,6},{5,7},{10,8},{15,9},{12,... | collective-permute-start | bytes 1376264 | tf_op jit(solution)/shard_map/ppermute | solution.py:42
  117.8 24.8 %all-to-all-start.3 = ((f32[256,1,128]{2,1,0:T(1,128)}), f32[256,1,128]{2,1,0:T(1,128)S(1)}, u32[]{:S(2)}, u32[]{:S(2)}) async-start(f32[256,1,128]{2,1,0:T(1,128)} %bitcast.60), calls=%async_computation.3 | async-start | bytes 262144 | tf_op jit(solution)/shard_map/all_to_all | solution.py:435
  142.6 0.7 copy-start.4
